TPU v7x, 32 devices: a whole 2x2x4 slice. The times are simulated.
32 devices in a mesh: ctx: 4 (over x, core), exp: 8 (over z, y).
Axes of the slice: x: 2, y: 2, z: 4, core: 2. Of those that a mesh axis runs over, the one named last changes fastest.
Arguments:
- inputs: bfloat16 [8, 1536, 768], P('exp', 'ctx'), may hold values from -6 to 6
- segments: int32 [8, 1536], P('exp', 'ctx'), may hold values from 0 to 15, as said below
- routes: int32 [8, 1536, 1], P('exp', 'ctx'), may hold values from 0 to 7; in each aligned block of 384 rows (0 to 383, 384 to 767, ..., all dimensions but the last counted through in order) at most 60 rows name the same one
- cotangent: bfloat16 [8, 1536, 768], P('exp', 'ctx'), may hold values from -6 to 6
- norm_gain: bfloat16 [768], P(('ctx', 'exp')), may hold values from 0.5 to 1.5
- in_proj: bfloat16 [768, 3072], P(('ctx', 'exp')), may hold values from -0.21875 to 0.21875
- conv_taps: bfloat16 [1536, 4], P(('ctx', 'exp')), may hold values from -3 to 3
- conv_bias: bfloat16 [1536], P(('ctx', 'exp')), may hold values from -1.5 to 1.5
- x_proj: bfloat16 [1536, 80], P(('ctx', 'exp')), may hold values from -0.15625 to 0.15625
- dt_proj: bfloat16 [48, 1536], P(None, ('ctx', 'exp')), may hold values from -0.875 to 0.875
- dt_bias: bfloat16 [1536], P(('ctx', 'exp')), may hold values from -5.5 to -3.5
- log_decay: bfloat16 [1536, 16], P(('ctx', 'exp')), may hold values from -4 to 1.1953125
- skip_gain: bfloat16 [1536], P(('ctx', 'exp')), may hold values from 0.5 to 1.5
- out_proj: bfloat16 [1536, 768], P(('ctx', 'exp')), may hold values from -0.3125 to 0.3125
- moe_gain: bfloat16 [768], P(('ctx', 'exp')), may hold values from 0.5 to 1.5
- router: bfloat16 [768, 8], P(('ctx', 'exp')), may hold values from -0.15625 to 0.15625
- expert_in: bfloat16 [8, 768, 3072], P('exp', None, 'ctx'), may hold values from -0.21875 to 0.21875
- expert_out: bfloat16 [8, 3072, 768], P('exp', 'ctx'), may hold values from -0.875 to 0.875
Outputs:
- outputs: bfloat16 [8, 1536, 768], P('exp', 'ctx')
- grad_inputs: float32 [8, 1536, 768], P('exp', 'ctx')
- grad_norm_gain: float32 [768], P(('ctx', 'exp'))
- grad_in_proj: float32 [768, 3072], P(('ctx', 'exp'))
- grad_conv_taps: float32 [1536, 4], P(('ctx', 'exp'))
- grad_conv_bias: float32 [1536], P(('ctx', 'exp'))
- grad_x_proj: float32 [1536, 80], P(('ctx', 'exp'))
- grad_dt_proj: float32 [48, 1536], P(None, ('ctx', 'exp'))
- grad_dt_bias: float32 [1536], P(('ctx', 'exp'))
- grad_log_decay: float32 [1536, 16], P(('ctx', 'exp'))
- grad_skip_gain: float32 [1536], P(('ctx', 'exp'))
- grad_out_proj: float32 [1536, 768], P(('ctx', 'exp'))
- grad_moe_gain: float32 [768], P(('ctx', 'exp'))
- grad_router: float32 [768, 8], P(('ctx', 'exp'))
- grad_expert_in: float32 [8, 768, 3072], P('exp', None, 'ctx')
- grad_expert_out: float32 [8, 3072, 768], P('exp', 'ctx')
Inputs may be any that keep to these rules, and one draw needn't show every extreme that they name: `segments`: segment numbers start at 0 and never fall along a sequence; each sequence holds one document that begins among its first 192 positions and ends within its last 192 positions, and each sequence's last document is number 16 - 1. `routes`: among the tokens of one device (aligned blocks of 384 positions), no expert is named more than 60 times, and some expert exactly that many.
All inputs are finite; a program needn't handle non-finite values.
Results may differ from a plain program's by a relative error of at most 0.017.
Values may be sent and summed in bfloat16 or wider, within the bound.
A program may use at most 192 MiB of HBM per device.

v0:
```python
import functools

import jax
import jax.numpy as jnp
from jax import lax
from jax.experimental import pallas as pl
from jax.experimental.pallas import tpu as pltpu
from jax.sharding import PartitionSpec as P

D = 768
DI = 1536
NS = 16
R = 48
KC = 4
LANES = 128
UNROLL = 8
LOG2E = 1.4426950408889634


EPS = 1e-05
MESH = pl.DeviceIdType.MESH
ROWS_AT_ONCE = 16
EDGE = 16

def tile(ref, base, lanes):
    return ref[pl.ds(pl.multiple_of(base, UNROLL), UNROLL), lanes]

def row(rows_now, place):
    return jnp.broadcast_to(rows_now[place : place + 1], (NS, LANES))

def cost(tokens, channels, share):
    size = tokens * channels * NS
    return pl.CostEstimate(flops=size * share, transcendentals=size, bytes_accessed=size * share)


def pick(channels):
    return 512 if channels % 512 == 0 else 128


def bit_positions(sizes):
    return [(axis, size.bit_length() - 2 - k) for axis, size in sizes for k in range(size.bit_length() - 1)]


def own_bit(place):
    axis, level = place
    return lax.rem(lax.axis_index(axis) // 2**level, 2)


def partner(place):
    axis, level = place
    where = {"ctx": lax.axis_index("ctx"), "exp": lax.axis_index("exp")}
    where[axis] = where[axis] + (1 - 2 * own_bit(place)) * 2**level
    return (where["ctx"], where["exp"])


def meet(places, *others):
    barrier = pltpu.get_barrier_semaphore()
    for device in [partner(place) for place in places] + list(others):
        pl.semaphore_signal(barrier, inc=1, device_id=device, device_id_type=MESH)
    pl.semaphore_wait(barrier, len(places) + len(others))


class GatherFlow:
    def __init__(self, places, streams, dims, shards, wholes, send_sems, recv_sems, local_sems):
        self.places, self.streams, self.dims, self.shards, self.wholes = places, streams, dims, shards, wholes
        self.sems = send_sems, recv_sems, local_sems
        self.bits = [own_bit(place) for place in places]

    def view(self, number, have):
        array, cols, order, begin = self.streams[number]
        index = tuple(slice(None) if p in have else self.bits[p] for p in self.dims)
        return self.wholes[array].at[index + (slice(None), cols)]

    def shard(self, number):
        array, cols, order, begin = self.streams[number]
        return self.shards[array].at[(slice(None),) * (begin + 1) + (cols,)]

    def own(self, number):
        array, cols, order, begin = self.streams[number]
        return pltpu.make_async_copy(self.shard(number), self.view(number, order[:begin]), self.sems[2].at[number])

    def flight(self, number, stage):
        array, cols, order, begin = self.streams[number]
        target = self.view(number, order[: begin + stage])
        return pltpu.make_async_remote_copy(
            src_ref=self.shard(number) if stage == 0 else target,
            dst_ref=target,
            send_sem=self.sems[0].at[number, stage],
            recv_sem=self.sems[1].at[number, stage],
            device_id=partner(self.places[order[begin + stage]]),
            device_id_type=MESH,
        )

    def stages(self, number):
        array, cols, order, begin = self.streams[number]
        return len(order) - begin

    def start(self):
        for number in range(len(self.streams)):
            self.flight(number, 0).start()
        for number in range(len(self.streams)):
            self.own(number).start()

    def advance(self, stage):
        for number in range(len(self.streams)):
            if stage >= self.stages(number):
                continue
            if stage == 0:
                self.own(number).wait()
            self.flight(number, stage).wait_recv()
            if stage + 1 < self.stages(number):
                self.flight(number, stage + 1).start()

    def finish(self):
        for number in range(len(self.streams)):
            for stage in range(self.stages(number)):
                self.flight(number, stage).wait_send()


def pack_small(small, square, channel_pack, width_pack):
    x_ref, dt_ref, taps_ref, decay_ref, vector_ref, pair_ref, router_ref = small
    rows, thin = channel_pack.shape[0], width_pack.shape[0]

    def laid(*pieces):
        square[...] = jnp.zeros_like(square)
        for first, ref in pieces:
            square[first : first + ref.shape[0], : ref.shape[1]] = ref[...].astype(jnp.float32)
        return square[...]

    dt_part = pltpu.roll(laid((0, dt_ref)).T, R + 2 * NS, 1)
    mix = laid((0, x_ref)) + dt_part
    channel_pack[:, :LANES] = mix[:rows].astype(jnp.bfloat16)
    turned_rows = laid((0, taps_ref), (8, decay_ref), (24, vector_ref)).T
    channel_pack[:, LANES:] = turned_rows[:rows].astype(jnp.bfloat16)
    width_pack[...] = laid((0, pair_ref), (8, router_ref)).T[:thin].astype(jnp.bfloat16)


def gather_kernel(places, streams, extra_streams, far, *refs):
    small = refs[:7]
    in_ref, out_ref, rows_ref, ids_ref, leaving = refs[7:12]
    extra = 2
    wholes, prior_ref, prior_ids, arriving = refs[12:17], refs[17], refs[18], refs[19]
    (square, channel_pack, width_pack, send_sems, recv_sems, local_sems, late_send, late_recv, late_local,
     edge_sems, moved_sems) = refs[20:]
    split = in_ref.shape[1] // 2
    shards = (in_ref.at[:, :split], channel_pack, width_pack, in_ref.at[:, split:], out_ref)
    pack_small(small, square, channel_pack, width_pack)
    count = 3
    flow = GatherFlow(
        places, streams, range(len(places)), shards[:count], wholes[:count], send_sems, recv_sems, local_sems
    )
    late = GatherFlow(
        places, extra_streams, far, shards[count:], wholes[count:], late_send, late_recv, late_local
    )
    blocks = lax.axis_size("ctx")
    here, line = lax.axis_index("ctx"), lax.axis_index("exp")
    meet(places, (lax.rem(here + 1, blocks), line), (lax.rem(here + blocks - 1, blocks), line))
    flow.start()
    tokens = rows_ref.shape[0]
    edges = [
        pltpu.make_async_remote_copy(
            src_ref=source,
            dst_ref=target,
            send_sem=edge_sems.at[0, k],
            recv_sem=edge_sems.at[1, k],
            device_id=(lax.rem(here + 1, blocks), line),
            device_id_type=MESH,
        )
        for k, (source, target) in enumerate(
            (
                (rows_ref.at[pl.ds(tokens - EDGE, EDGE)], prior_ref),
                (ids_ref.at[:, pl.ds(tokens - LANES, LANES)], prior_ids),
            )
        )
    ]
    for edge in edges:
        edge.start()
    move = row_half(leaving, arriving, moved_sems, ("ctx", blocks.bit_length() - 2), 0)
    move.start()
    stages, behind = len(places), len(far)
    for stage in range(stages):
        flow.advance(stage)
        if stage == behind - 2:
            late.start()
        if stage >= behind and stage - behind < behind:
            late.advance(stage - behind)
    for stage in range(stages - behind, behind):
        late.advance(stage)
    flow.finish()
    late.finish()
    for edge in edges:
        edge.wait()
    move.wait()


def orders_of(places):
    core = places.index(("ctx", 0))
    rows = [k for k, place in enumerate(places) if place[0] == "ctx" and place[1] > 0]
    near = places.index(("exp", 0))
    return [core] + rows + [near] + far_of(places), [core, near] + rows + far_of(places)


def far_of(places):
    return [k for k, place in sorted(enumerate(places), key=lambda item: item[1][1]) if place[0] == "exp" and place[1] > 0]


def halves(arrays, first, second, begin=None):
    streams = []
    for array, values in enumerate(arrays):
        width = values.shape[-1]
        rest = () if begin is None else (begin,)
        if width % (2 * LANES) == 0:
            count = 4 if width % (4 * LANES) == 0 and width >= 1024 else 2
            for k in range(count):
                part = (k % 2) * (count // 2) + k // 2
                cols = slice(part * width // count, (part + 1) * width // count)
                streams.append((array, cols, second if k % 2 else first) + rest)
        else:
            streams.append((array, slice(0, width), first if array % 2 else second) + rest)
    return streams


def gather_orders(places):
    return [tuple(reversed(order)) for order in orders_of(places)]


def gather_all(sizes, small, in_proj, out_proj, rows_in, ids, leaving, identity):
    places = bit_positions(sizes)
    stages = len(places)
    far = sorted(far_of(places))
    half = jnp.bfloat16
    rows, thin, split = small[0].shape[0], in_proj.shape[0], in_proj.shape[1] // 2
    shape = jax.ShapeDtypeStruct
    shards = shape((thin, split), half), shape((rows, 2 * LANES), half), shape((thin, LANES), half)
    extra = shape((thin, split), half), shape(out_proj.shape, half)
    streams = halves(shards, *gather_orders(places), begin=0)
    late = [(k, slice(0, part.shape[1]), tuple(reversed(far_of(places))), 0) for k, part in enumerate(extra)]
    anywhere = pl.BlockSpec(memory_space=pl.ANY)
    inside = pl.BlockSpec(memory_space=pltpu.VMEM)
    out = pl.pallas_call(
        functools.partial(gather_kernel, places, streams, late, far),
        in_specs=[inside] * 7 + [anywhere] * 5,
        out_specs=[anywhere] * 8,
        out_shape=[shape((2,) * stages + shard.shape, half) for shard in shards]
        + [shape((2,) * len(far) + part.shape, half) for part in extra]
        + [shape((EDGE, rows_in.shape[1]), half), shape((1, LANES), jnp.int32), shape(leaving.shape, half)],
        scratch_shapes=[
            pltpu.VMEM((LANES, LANES), jnp.float32),
            pltpu.VMEM((rows, 2 * LANES), half),
            pltpu.VMEM((thin, LANES), half),
            pltpu.SemaphoreType.DMA((len(streams), stages)),
            pltpu.SemaphoreType.DMA((len(streams), stages)),
            pltpu.SemaphoreType.DMA((len(streams),)),
            pltpu.SemaphoreType.DMA((len(late), len(far))),
            pltpu.SemaphoreType.DMA((len(late), len(far))),
            pltpu.SemaphoreType.DMA((len(late),)),
            pltpu.SemaphoreType.DMA((2, 2)),
            pltpu.SemaphoreType.DMA((2, 2)),
        ],
        compiler_params=pltpu.CompilerParams(
            collective_id=identity, has_side_effects=True, vmem_limit_bytes=63 * 1024 * 1024
        ),
        name="gather_all",
    )(*small, in_proj, out_proj, rows_in, ids, leaving)
    return [whole.reshape((-1,) + whole.shape[stages + 1 :]) for whole in out[:3]], out[3:5], out[7], out[5], out[6]


class ReduceFlow:
    def __init__(self, places, streams, dims, parts, totals, landing, send_sems, recv_sems):
        self.places, self.streams, self.dims, self.parts, self.totals = places, streams, dims, parts, totals
        self.landing, self.sems = landing, (send_sems, recv_sems)
        self.bits = [own_bit(place) for place in places]
        self.first = []
        for array, cols, order in streams:
            self.first.append(sum(len(other[2]) for other in streams[: len(self.first)]))

    def spot(self, number, stage):
        return self.landing[self.first[number] + stage]

    def side(self, number, stage, value):
        array, cols, order = self.streams[number]
        left = [p for p in self.dims if p not in order[:stage]]
        index = tuple(value if p == order[stage] else slice(None) for p in left)
        if stage == 0:
            return self.parts[array].at[index + (slice(None), cols)]
        return self.spot(number, stage - 1).at[index]

    def flight(self, number, stage):
        order = self.streams[number][2]
        return pltpu.make_async_remote_copy(
            src_ref=self.side(number, stage, 1 - self.bits[order[stage]]),
            dst_ref=self.spot(number, stage),
            send_sem=self.sems[0].at[number, stage],
            recv_sem=self.sems[1].at[number, stage],
            device_id=partner(self.places[order[stage]]),
            device_id_type=MESH,
        )

    def start(self):
        for number in range(len(self.streams)):
            self.flight(number, 0).start()

    def advance(self, stage):
        for number, (array, cols, order) in enumerate(self.streams):
            if stage >= len(order):
                continue
            self.flight(number, stage).wait_recv()
            mine = self.side(number, stage, self.bits[order[stage]])
            there = self.spot(number, stage)
            depth = len(self.dims) - stage - 1
            final = stage + 1 == len(order)
            if depth == 0:
                self.totals[array][:, cols] = there[...].astype(jnp.float32) + mine[...].astype(jnp.float32)
                continue

            def add(index, unused, there=there, mine=mine, depth=depth, final=final, array=array, cols=cols):
                at = tuple(lax.rem(index // 2 ** (depth - 1 - k), 2) for k in range(depth))
                value = there[at] + mine[at]
                if final:
                    self.totals[array][at + (slice(None), cols)] = value
                else:
                    there[at] = value
                return unused

            lax.fori_loop(0, 2**depth, add, 0)
            if not final:
                self.flight(number, stage + 1).start()

    def finish(self):
        for number in range(len(self.streams)):
            for stage in range(len(self.streams[number][2])):
                self.flight(number, stage).wait_send()


def landing_of(streams, dims, divided):
    landing = []
    for array, cols, order in streams:
        for stage in range(len(order)):
            rows = divided[array].shape[-2]
            landing.append(pltpu.VMEM((2,) * (len(dims) - stage - 1) + (rows, cols.stop - cols.start), jnp.bfloat16))
    return landing


def flights(streams):
    shape = (len(streams), max(len(order) for array, cols, order in streams))
    return [pltpu.SemaphoreType.DMA(shape)] * 2


def dot(left, right):
    return jnp.dot(left, right, preferred_element_type=jnp.float32)


def contract(left, right, left_dim, right_dim):
    return lax.dot_general(left, right, (((left_dim,), (right_dim,)), ((), ())), preferred_element_type=jnp.float32)


def lanes_of(group, width, k):
    return pl.ds(pl.multiple_of(group * width + k * LANES, LANES), LANES)


def spread_columns(source_ref, wide_ref):
    def chunk(index, unused):
        base = pl.multiple_of(index * LANES, LANES)
        now = source_ref[:, pl.ds(base, LANES)]
        for place in range(LANES):
            wide_ref[base + place] = jnp.broadcast_to(now[:, place : place + 1], (NS, LANES))
        return unused

    lax.fori_loop(0, source_ref.shape[1] // LANES, chunk, 0)


def end_pass(width, step_ref, push_ref, wide_b, rate_ref, state_ref, hook):
    rows, channels = step_ref.shape
    count = width // LANES

    def group_body(group, unused):
        pieces = [lanes_of(group, width, k) for k in range(count)]
        rates = [rate_ref[:, lanes] for lanes in pieces]

        def block(index, states):
            states = list(states)
            steps = [tile(step_ref, index * UNROLL, lanes) for lanes in pieces]
            pushes = [tile(push_ref, index * UNROLL, lanes) for lanes in pieces]
            for place in range(UNROLL):
                b_now = wide_b[index * UNROLL + place]
                for k in range(count):
                    decay = jnp.exp2(row(steps[k], place) * rates[k])
                    states[k] = decay * states[k] + b_now * row(pushes[k], place)
            return tuple(states)

        zero = jnp.zeros((NS, LANES), jnp.float32)
        states = lax.fori_loop(0, rows // UNROLL, block, (zero,) * count)
        for k, lanes in enumerate(pieces):
            state_ref[:, lanes] = states[k]
        hook(group)
        return unused

    lax.fori_loop(0, channels // width, group_body, 0)


def out_pass(width, step_ref, push_ref, wide_b, wide_c, rate_ref, state_ref, y_ref, kept_buf, kept_copy, hook):
    rows, channels = step_ref.shape
    count = width // LANES
    span = kept_buf.shape[1]
    blocks = rows // span

    def time_body(number, unused):
        slot = lax.rem(number, 2)

        @pl.when(number >= 2)
        def _():
            kept_copy(number - 2, slot).wait()

        def group_body(group, unused_inner):
            pieces = [lanes_of(group, width, k) for k in range(count)]
            rates = [rate_ref[:, lanes] for lanes in pieces]

            def block(index, states):
                states = list(states)
                base = number * span + index * UNROLL
                steps = [tile(step_ref, base, lanes) for lanes in pieces]
                pushes = [tile(push_ref, base, lanes) for lanes in pieces]
                trees = [Tree(True) for k in range(count)]
                for place in range(UNROLL):
                    b_now = wide_b[base + place]
                    c_now = wide_c[base + place]
                    for k, lanes in enumerate(pieces):
                        decay = jnp.exp2(row(steps[k], place) * rates[k])
                        states[k] = decay * states[k] + b_now * row(pushes[k], place)
                        kept_buf[slot, index * UNROLL + place, :, lanes] = states[k].astype(kept_buf.dtype)
                        trees[k].push(place, states[k] * c_now)
                for k, lanes in enumerate(pieces):
                    y_ref[pl.ds(pl.multiple_of(base, UNROLL), UNROLL), lanes] = trees[k].result
                return tuple(states)

            states = lax.fori_loop(0, span // UNROLL, block, tuple(state_ref[:, lanes] for lanes in pieces))
            for k, lanes in enumerate(pieces):
                state_ref[:, lanes] = states[k]
            return unused_inner

        lax.fori_loop(0, channels // width, group_body, 0)
        kept_copy(number, slot).start()
        hook(number)
        return unused

    lax.fori_loop(0, blocks, time_body, 0)
    for number in range(max(0, blocks - 2), blocks):
        kept_copy(number, number % 2).wait()


def inflow_pass(width, step_ref, grad_ref, wide_c, rate_ref, flow_ref, hook):
    rows, channels = step_ref.shape
    count = width // LANES

    def group_body(group, unused):
        hook(group)
        pieces = [lanes_of(group, width, k) for k in range(count)]
        rates = [rate_ref[:, lanes] for lanes in pieces]

        def block(index, flows):
            flows = list(flows)
            base = rows - UNROLL - index * UNROLL
            steps = [tile(step_ref, base, lanes) for lanes in pieces]
            grads = [tile(grad_ref, base, lanes) for lanes in pieces]
            for place in reversed(range(UNROLL)):
                c_now = wide_c[base + place]
                for k in range(count):
                    decay = jnp.exp2(row(steps[k], place) * rates[k])
                    flows[k] = decay * (c_now * row(grads[k], place) + flows[k])
            return tuple(flows)

        zero = jnp.zeros((NS, LANES), jnp.float32)
        flows = lax.fori_loop(0, rows // UNROLL, block, (zero,) * count)
        for k, lanes in enumerate(pieces):
            flow_ref[:, lanes] = flows[k]
        return unused

    lax.fori_loop(0, channels // width, group_body, 0)


class Tree:
    def __init__(self, rising):
        self.rising, self.held, self.result = rising, {}, None

    def push(self, place, value):
        now = value[:UNROLL] + value[UNROLL:]
        level = 0
        while 1 << level < UNROLL:
            if (place >> level) % 2 == (0 if self.rising else 1):
                self.held[level] = now
                return
            first, second = (self.held[level], now) if self.rising else (now, self.held[level])
            now = self.merge(first, second, 1 << level)
            level += 1
        self.result = now

    def merge(self, first, second, distance):
        low = (lax.broadcasted_iota(jnp.int32, (UNROLL, LANES), 0) & distance) == 0
        keep = jnp.where(low, first, second)
        give = jnp.where(low, second, first)
        other = pltpu.roll(give, distance, 0)
        if 2 * distance != UNROLL:
            other = jnp.where(low, pltpu.roll(give, UNROLL - distance, 0), other)
        return keep + other


def lane_sums(part_ref):
    values = part_ref[...].reshape(-1, LANES).astype(jnp.bfloat16)
    return contract(jnp.ones((UNROLL, LANES), jnp.bfloat16), values, 1, 1)


def adjoint_pass(width, step_ref, push_ref, grad_ref, wide_b, wide_c, rate_ref, flow_ref, kept_buf, kept_copy,
                 along_ref, slope_ref, gb_ref, gc_ref, ga_ref, part_b, part_c, hook):
    rows, channels = step_ref.shape
    count = width // LANES
    span = kept_buf.shape[1] - 1
    blocks = rows // span
    ga_ref[...] = jnp.zeros_like(ga_ref)

    def time_body(order, unused):
        slot = lax.rem(order, 2)
        number = blocks - 1 - order
        kept_copy(number, slot).wait()
        part_b[...] = jnp.zeros_like(part_b)
        part_c[...] = jnp.zeros_like(part_c)

        def group_body(group, unused_inner):
            pieces = [lanes_of(group, width, k) for k in range(count)]
            rates = [rate_ref[:, lanes] for lanes in pieces]

            def block(index, carried):
                flows = list(carried[:count])
                sums = list(carried[count : 2 * count])
                current = list(carried[2 * count :])
                local = span - UNROLL - index * UNROLL
                base = number * span + local
                steps = [tile(step_ref, base, lanes) for lanes in pieces]
                pushes = [tile(push_ref, base, lanes) for lanes in pieces]
                grads = [tile(grad_ref, base, lanes) for lanes in pieces]
                alongs = [Tree(False) for k in range(count)]
                slopes = [Tree(False) for k in range(count)]
                for place in reversed(range(UNROLL)):
                    b_now = wide_b[base + place]
                    c_now = wide_c[base + place]
                    gb = gc = None
                    for k, lanes in enumerate(pieces):
                        prior = kept_buf[slot, local + place, :, lanes].astype(jnp.float32)
                        step = row(steps[k], place)
                        grad = row(grads[k], place)
                        decay = jnp.exp2(step * rates[k])
                        adjoint = c_now * grad + flows[k]
                        flows[k] = decay * adjoint
                        decay_grad = flows[k] * prior
                        alongs[k].push(place, adjoint * b_now)
                        slopes[k].push(place, decay_grad * rates[k])
                        sums[k] = sums[k] + decay_grad * step
                        here_b = adjoint * row(pushes[k], place)
                        here_c = current[k] * grad
                        gb = here_b if gb is None else gb + here_b
                        gc = here_c if gc is None else gc + here_c
                        current[k] = prior
                    part_b[local + place] += gb
                    part_c[local + place] += gc
                where = pl.ds(pl.multiple_of(base, UNROLL), UNROLL)
                for k, lanes in enumerate(pieces):
                    along_ref[where, lanes] = alongs[k].result
                    slope_ref[where, lanes] = slopes[k].result
                return tuple(flows + sums + current)

            carried = lax.fori_loop(
                0,
                span // UNROLL,
                block,
                tuple(flow_ref[:, lanes] for lanes in pieces)
                + tuple(ga_ref[:, lanes] for lanes in pieces)
                + tuple(kept_buf[slot, span, :, lanes].astype(jnp.float32) for lanes in pieces),
            )
            for k, lanes in enumerate(pieces):
                flow_ref[:, lanes] = carried[k]
                ga_ref[:, lanes] = carried[count + k]
            return unused_inner

        lax.fori_loop(0, channels // width, group_body, 0)
        gb_ref[number] = lane_sums(part_b)
        gc_ref[number] = lane_sums(part_c)

        @pl.when(order + 2 < blocks)
        def _():
            kept_copy(number - 2, slot).start()

        hook(order)
        return unused

    lax.fori_loop(0, blocks, time_body, 0)


def share(source, target, send_sems, recv_sems):
    blocks = lax.axis_size("ctx")
    here, line = lax.axis_index("ctx"), lax.axis_index("exp")
    copies = []
    for step in range(1, blocks):
        copies.append(
            pltpu.make_async_remote_copy(
                src_ref=source,
                dst_ref=target.at[here],
                send_sem=send_sems.at[step],
                recv_sem=recv_sems.at[step],
                device_id=(lax.rem(here + step, blocks), line),
                device_id_type=MESH,
            )
        )
        copies[-1].start()
    target[here] = source[...]
    return copies


def row_peers():
    blocks = lax.axis_size("ctx")
    here, line = lax.axis_index("ctx"), lax.axis_index("exp")
    return [(lax.rem(here + step, blocks), line) for step in range(1, blocks)]


def row_half(source, target, sems, place, k):
    size = source.shape[0] // 2
    return pltpu.make_async_remote_copy(
        src_ref=source.at[pl.ds(k * size, size)],
        dst_ref=target.at[pl.ds(k * size, size)],
        send_sem=sems.at[0, k],
        recv_sem=sems.at[1, k],
        device_id=partner(place),
        device_id_type=MESH,
    )


def front(loaded, loads, room, outs, scratch, saves):
    normed_ref, bt_ref, ct_ref, rate_ref, chan_ref, gain_ref, delta_ref, same_ref, target_ref = outs
    nx, ext, conv, xs, pre, step, push = scratch
    in_ref, prior_ref, prior_ids, ids_ref, routes_ref, conv_w, channel_ref, width_ref = loaded
    for load in loads[:5] + loads[6:]:
        load.wait()
    tokens, channels = xs.shape
    width = in_ref.shape[1]
    mine = lax.axis_index("ctx")
    gain_rows = jnp.concatenate(
        [width_ref[at : at + LANES, :].astype(jnp.float32).T for at in range(0, width, LANES)], axis=1
    )
    gain_ref[...] = gain_rows[:8]
    for at in range(0, channels, LANES):
        chan_ref[:, at : at + LANES] = channel_ref[at : at + LANES, LANES:].astype(jnp.float32).T[:32]
    rate_ref[...] = -jnp.exp(chan_ref[8 : 8 + NS, :]) * LOG2E
    gain = gain_ref[0:1, :]

    def normed(values):
        x = values.astype(jnp.float32)
        return (x * lax.rsqrt(jnp.mean(x * x, axis=-1, keepdims=True) + EPS) * gain).astype(jnp.bfloat16)

    nx[:EDGE, :] = normed(prior_ref[...])

    def norm_rows(index, unused):
        at = pl.ds(pl.multiple_of(index * 16, 16), 16)
        value = normed(in_ref[at, :])
        normed_ref[at, :] = value
        nx[pl.ds(pl.multiple_of(EDGE + index * 16, 16), 16), :] = value
        return unused

    lax.fori_loop(0, tokens // 16, norm_rows, 0)
    def column(values):
        return jnp.broadcast_to(values.astype(jnp.float32), (LANES, LANES)).T

    def columns(ref):
        return jnp.concatenate([column(ref[:, at : at + LANES]) for at in range(0, tokens, LANES)], axis=0)

    ids = jnp.where(mine > 0, column(prior_ids[...])[LANES - EDGE :], -1.0)
    own_ids = columns(ids_ref)
    every_id = jnp.concatenate([ids, own_ids], axis=0)
    for j in range(1, KC):
        same_ref[j - 1] = (pltpu.roll(every_id, j, 0)[EDGE:] == own_ids).astype(jnp.float32)
    routes = columns(routes_ref)
    chosen = (routes == lax.broadcasted_iota(jnp.int32, routes.shape, 1).astype(jnp.float32)).astype(jnp.float32)
    square = (tokens, tokens)
    until = lax.broadcasted_iota(jnp.int32, square, 0) >= lax.broadcasted_iota(jnp.int32, square, 1)
    running = dot(until.astype(jnp.float32).astype(jnp.bfloat16), chosen.astype(jnp.bfloat16))
    slot = jnp.sum(running * chosen, axis=1, keepdims=True) - 1.0
    target_ref[...] = routes * room + slot
    piece = 2 * LANES
    loads[5].wait()

    def conv_piece(index, unused):
        lanes = pl.ds(pl.multiple_of(index * piece, piece), piece)
        low = dot(nx[...], conv_w[:, lanes]).astype(jnp.bfloat16)
        ext[:, lanes] = low
        value = low.astype(jnp.float32)
        out = chan_ref[24:25, lanes] + chan_ref[3:4, lanes] * value[EDGE:]
        for j in range(1, KC):
            same = jnp.concatenate([same_ref[j - 1]] * 2, axis=1)
            out = out + chan_ref[3 - j : 4 - j, lanes] * pltpu.roll(value, j, 0)[EDGE:] * same
        conv[:, lanes] = out
        xs[:, lanes] = (out / (1.0 + jnp.exp(-out))).astype(jnp.bfloat16)
        return unused

    lax.fori_loop(0, channels // piece, conv_piece, 0)
    for save in saves[:3]:
        save.start()
    projected = dot(xs[...], channel_ref[:, :LANES])
    lane = lax.broadcasted_iota(jnp.int32, projected.shape, 1)
    delta_ref[...] = jnp.where(lane >= R + 2 * NS, pltpu.roll(projected, R + 2 * NS, 1), 0.0).astype(jnp.bfloat16)
    for at in range(0, tokens, LANES):
        block = projected[at : at + LANES].T
        bt_ref[:, at : at + LANES] = block[R : R + NS]
        ct_ref[:, at : at + LANES] = block[R + NS : R + 2 * NS]

    def step_piece(index, unused):
        lanes = pl.ds(pl.multiple_of(index * piece, piece), piece)
        value = contract(delta_ref[...], channel_ref[lanes, :LANES], 1, 1) + chan_ref[25:26, lanes]
        pre[:, lanes] = value
        size = jnp.maximum(value, 0.0) + jnp.log1p(jnp.exp(-jnp.abs(value)))
        push[:, lanes] = size * xs[:, lanes].astype(jnp.float32)
        keep = jnp.concatenate([same_ref[0]] * 2, axis=1)
        step[:, lanes] = jnp.where(keep > 0, size, 1e30)
        return unused

    lax.fori_loop(0, channels // piece, step_piece, 0)
    for save in saves[3:]:
        save.start()


def forward_kernel(places, streams, width, room, *refs):
    weights_from = refs[:8]
    shards, leaving = refs[8:10], refs[10]
    y_ref, product_ref = refs[12:14]
    front_outs = refs[14:23]
    kept_ref = refs[23]
    saved = refs[24:30]
    wholes, arriving = refs[30:32], refs[32]
    scratch = refs[33:40]
    weights = refs[40:48]
    (wide_b, wide_c, kept_buf, first_buf, state_ref, message, products, ends,
     load_sems, kept_sems, first_sem, share_sems, save_sems, moved_sems, send_sems, recv_sems, local_sems) = refs[48:]
    loads = [pltpu.make_async_copy(weights_from[k], weights[k], load_sems.at[k]) for k in range(8)]
    for load in loads[:5] + loads[:4:-1]:
        load.start()
    bt_ref, ct_ref, rate_ref = front_outs[1:4]
    step_ref, push_ref = scratch[5:7]
    blocks = lax.axis_size("ctx")
    position = lax.axis_index("ctx")
    span = kept_buf.shape[1]
    flow = GatherFlow(places, streams, range(len(places)), shards, wholes, send_sems, recv_sems, local_sems)
    meet([place for place in places if place[0] == "exp"], *row_peers())
    flow.start()
    move = row_half(leaving, arriving, moved_sems, ("ctx", blocks.bit_length() - 2), 1)
    move.start()
    saves = [
        pltpu.make_async_copy(scratch[k + 1], saved[k], save_sems.at[k]) for k in range(6)
    ]
    front(weights, loads, room, front_outs, scratch, saves)

    message[0] = jnp.exp2(jnp.sum(step_ref[...], axis=0, keepdims=True) * rate_ref[...]).astype(jnp.bfloat16)
    early = share(message.at[0], products, share_sems.at[0], share_sems.at[1])
    spread_columns(bt_ref, wide_b)
    spread_columns(ct_ref, wide_c)
    end_pass(width, step_ref, push_ref, wide_b, rate_ref, state_ref, lambda group: None)
    message[1] = state_ref[...].astype(jnp.bfloat16)
    late = share(message.at[1], ends, share_sems.at[2], share_sems.at[3])
    flow.advance(0)
    for copy in early + late:
        copy.wait_recv()
    start = jnp.zeros(state_ref.shape, jnp.float32)
    for index in range(blocks):
        folded = products[index].astype(jnp.float32) * start + ends[index].astype(jnp.float32)
        start = jnp.where(index < position, folded, start)
    state_ref[...] = start
    product_ref[...] = products[...]
    first_buf[0] = start.astype(jnp.bfloat16)
    first_copy = pltpu.make_async_copy(first_buf, kept_ref.at[pl.ds(0, 1)], first_sem)
    first_copy.start()

    def kept_copy(number, slot):
        return pltpu.make_async_copy(
            kept_buf.at[slot], kept_ref.at[pl.ds(1 + number * span, span)], kept_sems.at[slot]
        )

    def hook(number):
        @pl.when(number == 3)
        def _():
            flow.advance(1)

    out_pass(width, step_ref, push_ref, wide_b, wide_c, rate_ref, state_ref, y_ref, kept_buf, kept_copy, hook)
    for stage in range(2, max(flow.stages(number) for number in range(len(streams)))):
        flow.advance(stage)
    flow.finish()
    first_copy.wait()
    for save in saves:
        save.wait()
    for copy in early + late:
        copy.wait_send()
    move.wait()


def scan_forward(sizes, rows_in, prior, ids, weights, room, shards, leaving, begun, identity, span=64):
    places = bit_positions(sizes)
    stages = len(places)
    begin = len(far_of(places))
    streams = halves(shards, *gather_orders(places), begin=begin)
    tokens, width = rows_in.shape
    channels = weights[0].shape[1]
    blocks = sizes[0][1]
    inside = pl.BlockSpec(memory_space=pltpu.VMEM)
    anywhere = pl.BlockSpec(memory_space=pl.ANY)
    half, full = jnp.bfloat16, jnp.float32
    shape = jax.ShapeDtypeStruct
    saved = [
        shape((EDGE + tokens, channels), half),
        shape((tokens, channels), full),
        shape((tokens, channels), half),
        shape((tokens, channels), full),
        shape((tokens, channels), full),
        shape((tokens, channels), full),
    ]
    y, products, normed, bt, ct, rates, chan, gains, delta, same, target, kept, *rest = pl.pallas_call(
        functools.partial(forward_kernel, places, streams, pick(channels), room),
        in_specs=[anywhere] * 12,
        input_output_aliases={11: 20},
        out_specs=[inside] * 11 + [anywhere] * 10,
        out_shape=[
            shape((tokens, channels), full),
            shape((blocks, NS, channels), half),
            shape((tokens, width), half),
            shape((NS, tokens), full),
            shape((NS, tokens), full),
            shape((NS, channels), full),
            shape((32, channels), full),
            shape((8, width), full),
            shape((tokens, LANES), half),
            shape((KC - 1, tokens, LANES), full),
            shape((tokens, LANES), full),
            shape((tokens + 1, NS, channels), half),
        ]
        + saved
        + [shape((2,) * stages + shard.shape[begin:], shard.dtype) for shard in shards]
        + [shape(leaving.shape, leaving.dtype)],
        scratch_shapes=[pltpu.VMEM((EDGE + tokens, width), half)]
        + [pltpu.VMEM(value.shape, value.dtype) for value in saved]
        + [pltpu.VMEM(value.shape, value.dtype) for value in [rows_in, *prior, *ids, *weights]]
        + [
            pltpu.VMEM((tokens, NS, LANES), full),
            pltpu.VMEM((tokens, NS, LANES), full),
            pltpu.VMEM((2, span, NS, channels), half),
            pltpu.VMEM((1, NS, channels), half),
            pltpu.VMEM((NS, channels), full),
            pltpu.VMEM((2, NS, channels), half),
            pltpu.VMEM((blocks, NS, channels), half),
            pltpu.VMEM((blocks, NS, channels), half),
            pltpu.SemaphoreType.DMA((8,)),
            pltpu.SemaphoreType.DMA((2,)),
            pltpu.SemaphoreType.DMA,
            pltpu.SemaphoreType.DMA((4, blocks)),
            pltpu.SemaphoreType.DMA((6,)),
            pltpu.SemaphoreType.DMA((2, 2)),
            pltpu.SemaphoreType.DMA((len(streams), stages)),
            pltpu.SemaphoreType.DMA((len(streams), stages)),
            pltpu.SemaphoreType.DMA((len(streams),)),
        ],
        compiler_params=pltpu.CompilerParams(
            collective_id=identity, has_side_effects=True, vmem_limit_bytes=63 * 1024 * 1024
        ),
        cost_estimate=cost(tokens, channels, 9),
        name="scan_forward",
    )(rows_in, *prior, *ids, *weights, *shards, leaving, begun)
    saved, wholes, arrived = rest[:6], rest[6:8], rest[8]
    wholes = [whole.reshape((-1,) + whole.shape[stages + 1 :]) for whole in wholes]
    return y, products, normed, bt, ct, rates, chan, gains, delta, same, target, kept, saved, wholes, arrived


def backward_kernel(places, streams, marks, width, *refs):
    bt_ref, ct_ref, rate_ref, product_ref = refs[:4]
    parts = refs[4:6]
    streamed = refs[6:9]
    kept_ref, leaving = refs[9:11]
    outs = refs[11:]
    gb_ref, gc_ref, ga_ref = outs[:3]
    totals, arriving = outs[3:5], outs[5]
    rows_out = outs[6:8]
    scratch = outs[8:]
    landing = scratch[:marks]
    (step_ref, push_ref, grad_ref, along_ref, slope_ref, wide_b, wide_c, part_b, part_c, kept_buf, flow_ref, message,
     inflows, load_sems, push_sem, out_sems, kept_sems, share_sems, moved_sems, send_sems, recv_sems) = scratch[marks:]
    blocks = lax.axis_size("ctx")
    position = lax.axis_index("ctx")
    span = kept_buf.shape[1] - 1
    steps = step_ref.shape[0] // span

    def load(group, k):
        lanes = pl.ds(pl.multiple_of(group * width, LANES), width)
        source, target = ((streamed[0], step_ref), (streamed[2], grad_ref))[k]
        return pltpu.make_async_copy(source.at[:, lanes], target.at[:, lanes], load_sems.at[k, group])

    for group in range(step_ref.shape[1] // width):
        for k in range(2):
            load(group, k).start()
    push_load = pltpu.make_async_copy(streamed[1], push_ref, push_sem)
    push_load.start()

    def ready(group):
        for k in range(2):
            load(group, k).wait()

    def rows_copy(number, k):
        rows = pl.ds(number * span, span)
        return pltpu.make_async_copy((along_ref, slope_ref)[k].at[rows], rows_out[k].at[rows], out_sems.at[k, number])

    flow = ReduceFlow(places, streams, range(len(places)), parts, totals, landing, send_sems, recv_sems)

    def kept_copy(number, slot):
        return pltpu.make_async_copy(
            kept_ref.at[pl.ds(number * span, span + 1)], kept_buf.at[slot], kept_sems.at[slot]
        )

    for order in range(min(2, steps)):
        kept_copy(steps - 1 - order, order).start()
    meet([place for place in places if place[0] == "exp"], *row_peers())
    flow.start()
    move = row_half(leaving, arriving, moved_sems, ("ctx", blocks.bit_length() - 2), 0)
    move.start()
    spread_columns(bt_ref, wide_b)
    spread_columns(ct_ref, wide_c)
    inflow_pass(width, step_ref, grad_ref, wide_c, rate_ref, flow_ref, ready)
    message[...] = flow_ref[...].astype(jnp.bfloat16)
    copies = share(message, inflows, share_sems.at[0], share_sems.at[1])
    for copy in copies:
        copy.wait_recv()
    end = jnp.zeros(flow_ref.shape, jnp.float32)
    for index in reversed(range(blocks)):
        folded = inflows[index].astype(jnp.float32) + product_ref[index].astype(jnp.float32) * end
        end = jnp.where(index > position, folded, end)
    flow_ref[...] = end
    flow.advance(0)
    push_load.wait()

    def hook(order):
        for k in range(2):
            rows_copy(steps - 1 - order, k).start()

        @pl.when(order == 2)
        def _():
            flow.advance(1)

        @pl.when(order == 4)
        def _():
            flow.advance(2)

    adjoint_pass(width, step_ref, push_ref, grad_ref, wide_b, wide_c, rate_ref, flow_ref, kept_buf, kept_copy,
                 along_ref, slope_ref, gb_ref, gc_ref, ga_ref, part_b, part_c, hook)
    for stage in range(3, len(streams[0][2])):
        flow.advance(stage)
    flow.finish()
    for copy in copies:
        copy.wait_send()
    move.wait()
    for number in range(steps):
        for k in range(2):
            rows_copy(number, k).wait()


def scan_backward(sizes, step, push, grad, b_turned, c_turned, rates, products, parts, kept, leaving, identity, span=64):
    places = bit_positions(sizes)
    stages = len(places)
    far = sorted(far_of(places))
    streams = halves(parts, *[tuple(order[: stages - len(far)]) for order in orders_of(places)])
    divided = [part.reshape((2,) * stages + (-1, part.shape[1])) for part in parts]
    tokens, channels = step.shape
    blocks = sizes[0][1]
    inside = pl.BlockSpec(memory_space=pltpu.VMEM)
    anywhere = pl.BlockSpec(memory_space=pl.ANY)
    half = jnp.bfloat16
    landing = landing_of(streams, range(stages), divided)
    row_sums = jax.ShapeDtypeStruct((tokens // span, UNROLL, span * NS), jnp.float32)
    out = pl.pallas_call(
        functools.partial(backward_kernel, places, streams, len(landing), pick(channels)),
        in_specs=[inside] * 6 + [anywhere] * 5,
        out_specs=[inside] * 5 + [anywhere] * 3,
        out_shape=[row_sums, row_sums, jax.ShapeDtypeStruct((NS, channels), jnp.float32)]
        + [jax.ShapeDtypeStruct((2,) * len(far) + block.shape[-2:], half) for block in divided]
        + [jax.ShapeDtypeStruct(leaving.shape, leaving.dtype)]
        + [jax.ShapeDtypeStruct((tokens, channels), jnp.float32)] * 2,
        scratch_shapes=landing
        + [pltpu.VMEM((tokens, channels), jnp.float32)] * 5
        + [
            pltpu.VMEM((tokens, NS, LANES), jnp.float32),
            pltpu.VMEM((tokens, NS, LANES), jnp.float32),
            pltpu.VMEM((span, NS, LANES), jnp.float32),
            pltpu.VMEM((span, NS, LANES), jnp.float32),
            pltpu.VMEM((2, span + 1, NS, channels), half),
            pltpu.VMEM((NS, channels), jnp.float32),
            pltpu.VMEM((NS, channels), half),
            pltpu.VMEM((blocks, NS, channels), half),
            pltpu.SemaphoreType.DMA((2, channels // pick(channels))),
            pltpu.SemaphoreType.DMA,
            pltpu.SemaphoreType.DMA((2, tokens // span)),
            pltpu.SemaphoreType.DMA((2,)),
            pltpu.SemaphoreType.DMA((2, blocks)),
            pltpu.SemaphoreType.DMA((2, 2)),
        ]
        + flights(streams),
        compiler_params=pltpu.CompilerParams(
            collective_id=identity, has_side_effects=True, vmem_limit_bytes=63 * 1024 * 1024
        ),
        cost_estimate=cost(tokens, channels, 15),
        name="scan_backward",
    )(b_turned, c_turned, rates, products, *divided, step, push, grad, kept, leaving)
    wide_b, wide_c, grad_a, first, second, arrived, along, slope = out
    grad_bs, grad_cs = [values[:, 0].reshape(tokens, NS) for values in (wide_b, wide_c)]
    return along, slope, grad_bs, grad_cs, grad_a, (first, second), arrived


class PackedReduce(ReduceFlow):
    def __init__(self, places, streams, heads, parts, totals, landing, blocks, send_sems, recv_sems):
        super().__init__(places, streams, range(len(places)), parts, totals, landing, send_sems, recv_sems)
        self.heads, self.blocks = heads, blocks

    def side(self, number, stage, value):
        array, cols, order = self.streams[number]
        if stage == 0:
            index = tuple(value if p == order[0] else slice(None) for p in range(self.heads))
            return self.parts[array].at[index + (slice(None), cols)]
        left = [p for p in self.dims if p not in order[:stage]]
        index = tuple(value if p == order[stage] else slice(None) for p in left)
        held = self.blocks[number] if stage == 1 else self.spot(number, stage - 1)
        return held.at[index]

    def advance(self, stage):
        if stage:
            super().advance(stage)
            return
        for number, (array, cols, order) in enumerate(self.streams):
            self.flight(number, 0).wait_recv()
            mine = self.side(number, 0, self.bits[order[0]])
            there, held = self.spot(number, 0), self.blocks[number]
            tails = len(self.places) - self.heads
            size = held.shape[-2]

            def add(index, unused, mine=mine, there=there, held=held, tails=tails, size=size):
                at = tuple(lax.rem(index // 2 ** (self.heads - 2 - k), 2) for k in range(self.heads - 1))
                value = there[at].astype(jnp.float32) + mine[at].astype(jnp.float32)
                for block in range(2**tails):
                    spot = tuple(block // 2 ** (tails - 1 - k) % 2 for k in range(tails))
                    held[at + spot] = value[block * size : (block + 1) * size].astype(held.dtype)
                return unused

            lax.fori_loop(0, 2 ** (self.heads - 1), add, 0)
            self.flight(number, 1).start()


def turned(values):
    return jnp.concatenate([values[:, at : at + LANES].T for at in range(0, values.shape[1], LANES)], axis=0)


def finish_kernel(places, streams, third, late, far, marks, *refs):
    leaving = refs[23:25]
    refs = refs[:23] + refs[27:]
    (along_h, slope_h, grad_h, pre_h, conv_h, xs_h, ext_h, gz_h, wc_h, wg_h) = refs[:10]
    (normed_ref, in_ref, resid_ref, mix_ref, bc_ref, delta_ref, same_ref, chan_ref, decay_ref, rate_ref, wide_ref) = refs[10:21]
    rest_parts = refs[21:23]
    gi_ref, own_in, own_out, tot_small, tot_wide = refs[23:28]
    arriving, scratch = refs[28:30], refs[30:]
    landing, scratch = scratch[: marks[0]], scratch[marks[0] :]
    blocks, scratch = scratch[: marks[1]], scratch[marks[1] :]
    landing3, scratch = scratch[: marks[2]], scratch[marks[2] :]
    blocks3, scratch = scratch[: marks[3]], scratch[marks[3] :]
    late_landing, scratch = scratch[: marks[4]], scratch[marks[4] :]
    (along, slope, grad, pre, conv, xs, ext, gz, wc, wg, gdt, gci, last, spill, arrived, sums, rows_s, wide_s, gn,
     part_conv, part_small, part_wide,
     block_sems, whole_sems, spill_sems, moved_sems, send_sems, recv_sems, send3, recv3, late_send, late_recv) = scratch
    tokens, channels = xs.shape
    own_conv, own_gate = own_in.at[:, :channels], own_in.at[:, channels:]
    span = tokens // block_sems.shape[1]
    heads = len([place for place in places if place[0] == "ctx"])
    flow = PackedReduce(
        places, streams, heads, (part_conv, part_small), (own_conv, tot_small), landing, blocks, send_sems, recv_sems
    )
    flow3 = PackedReduce(places, third, heads, (part_wide,), (tot_wide,), landing3, blocks3, send3, recv3)
    rest = ReduceFlow(places, late, far, rest_parts, (own_gate, own_out), late_landing, late_send, late_recv)

    streamed = ((along_h, along), (slope_h, slope), (grad_h, grad), (pre_h, pre), (xs_h, xs))

    def block_copy(k, number):
        rows = pl.ds(number * span, span)
        source, target = streamed[k]
        return pltpu.make_async_copy(source.at[rows], target.at[rows], block_sems.at[k, number])

    for number in range(tokens // span):
        for k in range(len(streamed)):
            block_copy(k, number).start()
    wholes = [
        pltpu.make_async_copy(source, target, whole_sems.at[k])
        for k, (source, target) in enumerate(((conv_h, conv), (ext_h, ext), (gz_h, gz), (wc_h, wc), (wg_h, wg)))
    ]
    for copy in wholes:
        copy.start()
    count = lax.axis_size("ctx")
    here, line = lax.axis_index("ctx"), lax.axis_index("exp")
    before = (lax.rem(here + count - 1, count), line)
    meet(places, before, (lax.rem(here + 1, count), line))
    rest.start()
    moves = [
        row_half(leaving[k], arriving[k], moved_sems.at[k], ("ctx", count.bit_length() - 2), 1) for k in range(2)
    ]
    moves[0].start()

    sums[...] = jnp.zeros_like(sums)
    rows_s[...] = jnp.zeros_like(rows_s)

    def first_block(number, unused):
        for k in range(len(streamed)):
            block_copy(k, number).wait()

        def some(index, unused_inner):
            at = pl.ds(pl.multiple_of(number * span + index * 16, 16), 16)
            for low in range(0, channels, LANES):
                lanes = slice(low, low + LANES)
                a, g, x, p = along[at, lanes], grad[at, lanes], xs[at, lanes].astype(jnp.float32), pre[at, lanes]
                small = jnp.exp(-jnp.abs(p))
                gated = jnp.where(p >= 0, 1.0, small) / (1.0 + small)
                step = jnp.maximum(p, 0.0) + jnp.log1p(small)
                value = (a * x + slope[at, lanes] * (1.0 / LOG2E)) * gated
                gdt[at, lanes] = value.astype(jnp.bfloat16)
                sums[0, :, lanes] += value[:8] + value[8:]
                both = g * x
                sums[1, :, lanes] += both[:8] + both[8:]
                along[at, lanes] = chan_ref[26:27, lanes] * g + a * step
            return unused_inner

        lax.fori_loop(0, span // 16, some, 0)
        return unused

    lax.fori_loop(0, tokens // span, first_block, 0)
    rows_s[25:26, :] = jnp.sum(sums[0], axis=0, keepdims=True)
    rows_s[26:27, :] = jnp.sum(sums[1], axis=0, keepdims=True)
    rows_s[8:24, :] = decay_ref[...] * rate_ref[...] * (1.0 / LOG2E)

    lane = lax.broadcasted_iota(jnp.int32, (tokens, LANES), 1)
    mixed = pltpu.roll(dot(gdt[...], mix_ref[:, :LANES]), R, 1)
    projected = jnp.where(lane < R, mixed, jnp.where(lane < R + 2 * NS, bc_ref[...], 0.0)).astype(jnp.bfloat16)
    wholes[0].wait()
    wholes[1].wait()
    piece = 2 * LANES
    tail_row = lax.broadcasted_iota(jnp.int32, (tokens, piece), 0)

    def conv_piece(index, unused):
        lanes = pl.ds(pl.multiple_of(index * piece, piece), piece)
        some = pl.ds(pl.multiple_of(index * piece, piece), piece)
        total = along[:, lanes] + contract(projected, mix_ref[some, :LANES], 1, 1)
        value = conv[:, lanes]
        gate = 1.0 / (1.0 + jnp.exp(-value))
        out = total * gate * (1.0 + value * (1.0 - gate))
        rows_s[24:25, lanes] = jnp.sum(out, axis=0, keepdims=True)
        before_rows = ext[:, lanes].astype(jnp.float32)
        rows_s[3:4, lanes] = jnp.sum(out * before_rows[EDGE:], axis=0, keepdims=True)
        result = chan_ref[3:4, lanes] * out
        beyond = jnp.zeros((8, piece), jnp.float32)
        for j in range(1, KC):
            same = jnp.concatenate([same_ref[j - 1]] * 2, axis=1)
            masked = out * same
            shifted_rows = pltpu.roll(before_rows, j, 0)[EDGE:]
            rows_s[3 - j : 4 - j, lanes] = jnp.sum(masked * shifted_rows, axis=0, keepdims=True)
            moved = chan_ref[3 - j : 4 - j, lanes] * pltpu.roll(masked, tokens - j, 0)
            result = result + jnp.where(tail_row < tokens - j, moved, 0.0)
            beyond = beyond + jnp.where(tail_row < tokens - j, 0.0, moved)[tokens - 8 :]
        gci[:, lanes] = result.astype(jnp.bfloat16)
        last[:, lanes] = result[tokens - 16 :]
        spill[:, lanes] = beyond
        return unused

    lax.fori_loop(0, channels // piece, conv_piece, 0)
    handed = pltpu.make_async_remote_copy(
        src_ref=spill,
        dst_ref=arrived,
        send_sem=spill_sems.at[0],
        recv_sem=spill_sems.at[1],
        device_id=before,
        device_id_type=MESH,
    )
    handed.start()

    cut = part_small.shape[-2]
    first_rows = contract(projected, xs[...], 0, 0) + contract(delta_ref[...], gdt[...], 0, 0)
    filler = jnp.zeros((LANES - rows_s.shape[0], channels), jnp.float32)
    for k, values in enumerate((first_rows, jnp.concatenate([rows_s[...], filler], axis=0))):
        columns = turned(values)
        for index in range(channels // cut):
            spot = tuple(index // 2 ** (heads - 1 - j) % 2 for j in range(heads))
            part_small[spot + (slice(None), slice(k * LANES, (k + 1) * LANES))] = columns[
                index * cut : (index + 1) * cut
            ].astype(jnp.bfloat16)
    handed.wait_recv()
    closing = last[...] + jnp.concatenate([jnp.zeros((8, channels), jnp.float32), arrived[...]], axis=0)
    gci[tokens - 16 :, :] = closing.astype(jnp.bfloat16)

    long = part_conv.shape[-2]

    def product_piece(index, unused):
        lanes = pl.ds(pl.multiple_of(index * piece, piece), piece)
        value = dot(normed_ref[...], gci[:, lanes])
        for block in range(value.shape[0] // long):
            spot = tuple(block // 2 ** (heads - 1 - k) % 2 for k in range(heads))
            part_conv[spot + (slice(None), lanes)] = value[block * long : (block + 1) * long].astype(jnp.bfloat16)
        return unused

    lax.fori_loop(0, channels // piece, product_piece, 0)
    flow.start()

    for copy in wholes[2:]:
        copy.wait()
    width = gn.shape[1]

    def normed_piece(index, unused):
        lanes = pl.ds(pl.multiple_of(index * piece, piece), piece)
        gn[:, lanes] = contract(gci[...], wc[lanes, :], 1, 1) + contract(gz[...], wg[lanes, :], 1, 1)
        return unused

    lax.fori_loop(0, width // piece, normed_piece, 0)
    wide_s[...] = wide_ref[...]
    gain = wide_ref[0:1, :]

    def back(index, total):
        at = pl.ds(pl.multiple_of(index * 16, 16), 16)
        x, g = in_ref[at, :].astype(jnp.float32), gn[at, :]
        scale = lax.rsqrt(jnp.mean(x * x, axis=-1, keepdims=True) + EPS)
        scaled = g * gain
        share_of = jnp.mean(x * scaled, axis=-1, keepdims=True)
        gi_ref[at, :] = resid_ref[at, :] + scale * scaled - x * (scale * scale * scale * share_of)
        value = g * (x * scale)
        return total + value[:8] + value[8:]

    total = lax.fori_loop(0, tokens // 16, back, jnp.zeros((8, width), jnp.float32))
    wide_s[0:1, :] = jnp.sum(total, axis=0, keepdims=True)
    flow.advance(0)
    filler = jnp.zeros((LANES - wide_s.shape[0], width), jnp.float32)
    columns = turned(jnp.concatenate([wide_s[...], filler], axis=0))
    short = part_wide.shape[-2]
    for block in range(width // short):
        spot = tuple(block // 2 ** (heads - 1 - k) % 2 for k in range(heads))
        part_wide[spot] = columns[block * short : (block + 1) * short].astype(jnp.bfloat16)
    flow3.start()
    rest.advance(0)
    for stage in range(1, len(places)):
        flow.advance(stage)
        flow3.advance(stage - 1)
        rest.advance(stage)
        if stage == 2:
            moves[1].start()
    flow3.advance(len(places) - 1)

    flow.finish()
    flow3.finish()
    rest.finish()
    handed.wait_send()
    for move in moves:
        move.wait()


def finish(sizes, streamed, inside_values, parts, leaving, arrived, identity, span=64):
    places = bit_positions(sizes)
    stages = len(places)
    far = sorted(far_of(places))
    heads = sizes[0][1].bit_length() - 1
    tails = stages - heads
    along, slope, grad, pre, conv, xs, ext, gz, wc, wg = streamed
    normed = inside_values[1]
    tokens, channels = xs.shape
    width = normed.shape[1]
    devices = 2**stages
    half, wide = jnp.bfloat16, jnp.float32
    rows, thin = channels // devices, width // devices
    orders = [tuple(order) for order in orders_of(places)]
    conv_like = jax.ShapeDtypeStruct((width, channels), half)
    small_like = jax.ShapeDtypeStruct((channels, 2 * LANES), half)
    wide_like = jax.ShapeDtypeStruct((width, LANES), half)
    streams = halves((conv_like, small_like), *orders)
    third = halves((wide_like,), *orders)
    late = [(k, slice(0, part.shape[-1]), tuple(far_of(places))) for k, part in enumerate(parts)]

    def room(of, sizes_of):
        landing, blocks = [], []
        for array, cols, order in of:
            size, many = sizes_of[array], cols.stop - cols.start
            landing.append(pltpu.VMEM((2,) * (heads - 1) + (size * 2**tails, many), half))
            landing += [pltpu.VMEM((2,) * (stages - stage - 1) + (size, many), half) for stage in range(1, stages)]
            blocks.append(pltpu.VMEM((2,) * (stages - 1) + (size, many), half))
        return landing, blocks

    landing, blocks = room(streams, (thin, rows))
    landing3, blocks3 = room(third, (thin,))
    late_landing = landing_of(late, far, parts)
    marks = [len(landing), len(blocks), len(landing3), len(blocks3), len(late_landing)]
    inside = pl.BlockSpec(memory_space=pltpu.VMEM)
    anywhere = pl.BlockSpec(memory_space=pl.ANY)
    return pl.pallas_call(
        functools.partial(finish_kernel, places, streams, third, late, far, marks),
        in_specs=[anywhere] * 10 + [inside] * (len(inside_values) + 2) + [anywhere] * 4,
        input_output_aliases={25: 5, 26: 6},
        out_specs=[inside] * 5 + [anywhere] * 2,
        out_shape=[
            jax.ShapeDtypeStruct(normed.shape, wide),
            jax.ShapeDtypeStruct((thin, 2 * channels), wide),
            jax.ShapeDtypeStruct(parts[1].shape[-2:], wide),
            jax.ShapeDtypeStruct((rows, 2 * LANES), wide),
            jax.ShapeDtypeStruct((thin, LANES), wide),
        ]
        + [jax.ShapeDtypeStruct(values.shape, half) for values in leaving],
        scratch_shapes=landing + blocks + landing3 + blocks3 + late_landing
        + [pltpu.VMEM(value.shape, value.dtype) for value in streamed]
        + [
            pltpu.VMEM((tokens, channels), half),
            pltpu.VMEM((tokens, channels), half),
            pltpu.VMEM((16, channels), wide),
            pltpu.VMEM((8, channels), wide),
            pltpu.VMEM((8, channels), wide),
            pltpu.VMEM((2, 8, channels), wide),
            pltpu.VMEM((32, channels), wide),
            pltpu.VMEM(inside_values[-1].shape, wide),
            pltpu.VMEM((tokens, width), wide),
            pltpu.VMEM((2,) * heads + (thin * 2**tails, channels), half),
            pltpu.VMEM((2,) * heads + (rows * 2**tails, 2 * LANES), half),
            pltpu.VMEM((2,) * heads + (thin * 2**tails, LANES), half),
            pltpu.SemaphoreType.DMA((5, tokens // span)),
            pltpu.SemaphoreType.DMA((5,)),
            pltpu.SemaphoreType.DMA((2,)),
            pltpu.SemaphoreType.DMA((2, 2, 2)),
        ]
        + flights(streams)
        + flights(third)
        + flights(late),
        compiler_params=pltpu.CompilerParams(
            collective_id=identity, has_side_effects=True, vmem_limit_bytes=63 * 1024 * 1024
        ),
        name="finish",
    )(*streamed, *inside_values, *parts, *leaving, *arrived)


def chosen_of(target, room):
    lane = lax.broadcasted_iota(jnp.int32, target.shape, 1).astype(jnp.float32) * room
    return ((target >= lane) & (target < lane + room)).astype(jnp.float32)


def gate_kernel(room, experts, y_ref, xs_ref, normed_ref, in_ref, cot_ref, target_ref, wg_ref, wo_ref, wide_ref, chan_ref,
                gain_ref, n2_ref, resid_ref, z_ref, prob_ref, pick_ref, gated_t, normed_t):
    skip, gain = chan_ref[26:27, :], gain_ref[1:2, :]
    gate_in = dot(normed_ref[...], wg_ref[...])
    z_ref[...] = gate_in
    scanned = y_ref[...] + skip * xs_ref[...].astype(jnp.float32)
    gated = scanned * gate_in / (1.0 + jnp.exp(-gate_in))
    for at in range(0, gated.shape[1], LANES):
        gated_t[at : at + LANES, :] = gated[:, at : at + LANES].T.astype(jnp.bfloat16)
    for at in range(0, normed_ref.shape[1], LANES):
        normed_t[at : at + LANES, :] = normed_ref[:, at : at + LANES].astype(jnp.float32).T.astype(jnp.bfloat16)
    residual = in_ref[...].astype(jnp.float32) + dot(gated.astype(jnp.bfloat16), wo_ref[...])
    resid_ref[...] = residual
    scale = lax.rsqrt(jnp.mean(residual * residual, axis=-1, keepdims=True) + EPS)
    normed_two = (residual * scale * gain).astype(jnp.bfloat16)
    n2_ref[...] = normed_two
    logits = pltpu.roll(dot(normed_two, wide_ref[...]), LANES - 8, 1)
    lane = lax.broadcasted_iota(jnp.int32, logits.shape, 1)
    logits = jnp.where(lane < experts, logits, -1e30)
    powers = jnp.exp(logits - jnp.max(logits, axis=1, keepdims=True))
    powers = jnp.where(lane < experts, powers, 0.0)
    probability = powers / jnp.sum(powers, axis=1, keepdims=True)
    prob_ref[...] = probability
    gate = jnp.sum(probability * chosen_of(target_ref[...], room), axis=1, keepdims=True)
    pick_ref[...] = (cot_ref[...].astype(jnp.float32) * gate).astype(jnp.bfloat16)


def open_gate(y, xs, normed, rows_in, cotangent, target, weights, room, experts, block=3 * LANES):
    tokens, channels = y.shape
    width = rows_in.shape[1]
    shape, half, full = jax.ShapeDtypeStruct, jnp.bfloat16, jnp.float32

    def cut(values):
        return pl.BlockSpec((block, values.shape[1]), lambda i: (i, 0))

    def whole(values):
        return pl.BlockSpec(values.shape, lambda i: (0, 0))

    results = [
        shape((tokens, width), half),
        shape((tokens, width), full),
        shape((tokens, channels), full),
        shape((tokens, LANES), full),
        shape((tokens, width), half),
    ]
    turned_specs = [pl.BlockSpec((rows, block), lambda i: (0, i)) for rows in (channels, width)]
    return pl.pallas_call(
        functools.partial(gate_kernel, room, experts),
        grid=(tokens // block,),
        in_specs=[cut(values) for values in (y, xs, normed, rows_in, cotangent, target)]
        + [whole(values) for values in weights],
        out_specs=[cut(values) for values in results] + turned_specs,
        out_shape=results + [shape((channels, tokens), half), shape((width, tokens), half)],
        compiler_params=pltpu.CompilerParams(vmem_limit_bytes=63 * 1024 * 1024),
        name="open_gate",
    )(y, xs, normed, rows_in, cotangent, target, *weights)


def middle_kernel(room, picked_ref, back_ref, cot_ref, resid_ref, z_ref, y_ref, xs_ref, n2_ref, prob_ref, target_ref,
                  gated_t, normed_t, wo_ref, wide_ref, chan_ref, gain_ref,
                  out_ref, gres_ref, gy_ref, gz_ref, rows_ref, sum_out, sum_gate, mix_all, gz_all):
    step, steps = pl.program_id(0), pl.num_programs(0)

    @pl.when(step == 0)
    def _():
        rows_ref[...] = jnp.zeros_like(rows_ref)
        rows_ref[0:1, :] = gain_ref[0:1, :]

    size = out_ref.shape[0]
    gain = gain_ref[1:2, :]
    grad, picked = cot_ref[...].astype(jnp.float32), picked_ref[...].astype(jnp.float32)
    probability, chosen = prob_ref[...], chosen_of(target_ref[...], room)
    gate = jnp.sum(probability * chosen, axis=1, keepdims=True)
    residual = resid_ref[...]
    out_ref[...] = (residual + gate * picked).astype(jnp.bfloat16)
    grad_gate = jnp.sum(grad * picked, axis=1, keepdims=True)
    grad_logits = probability * (grad_gate * (chosen - gate))
    shifted_logits = pltpu.roll(grad_logits, 8, 1).astype(jnp.bfloat16)
    grad_two = back_ref[...].astype(jnp.float32) + contract(shifted_logits, wide_ref[...], 1, 1)
    rows_ref[...] += contract(shifted_logits, n2_ref[...], 0, 0)[: rows_ref.shape[0]]
    scale = lax.rsqrt(jnp.mean(residual * residual, axis=-1, keepdims=True) + EPS)
    rows_ref[1:2, :] += jnp.sum(grad_two * residual * scale, axis=0, keepdims=True)
    scaled = grad_two * gain
    share_of = jnp.mean(residual * scaled, axis=-1, keepdims=True)
    total = grad + scale * scaled - residual * (scale * scale * scale * share_of)
    gres_ref[...] = total
    mix = total.astype(jnp.bfloat16)
    at = pl.ds(pl.multiple_of(step * size, size), size)
    mix_all[at, :] = mix
    grad_gated = contract(mix, wo_ref[...], 1, 1)
    value = z_ref[...]
    bend = 1.0 / (1.0 + jnp.exp(-value))
    gy_ref[...] = grad_gated * value * bend
    scanned = y_ref[...] + chan_ref[26:27, :] * xs_ref[...].astype(jnp.float32)
    grad_z = (grad_gated * scanned * bend * (1.0 + value * (1.0 - bend))).astype(jnp.bfloat16)
    gz_ref[...] = grad_z
    gz_all[at, :] = grad_z

    @pl.when(step == steps - 1)
    def _():
        piece = 2 * LANES

        def some(index, unused):
            lanes = pl.ds(pl.multiple_of(index * piece, piece), piece)
            sum_out[:, lanes] = dot(gated_t[...], mix_all[:, lanes]).astype(jnp.bfloat16)
            return unused

        def other(index, unused):
            lanes = pl.ds(pl.multiple_of(index * piece, piece), piece)
            sum_gate[:, lanes] = dot(normed_t[...], gz_all[:, lanes]).astype(jnp.bfloat16)
            return unused

        lax.fori_loop(0, sum_out.shape[1] // piece, some, 0)
        lax.fori_loop(0, sum_gate.shape[1] // piece, other, 0)


def middle(blocks, turned_parts, weights, room, experts, block=3 * LANES):
    tokens, width = blocks[0].shape
    channels = turned_parts[0].shape[0]
    shape, half, full = jax.ShapeDtypeStruct, jnp.bfloat16, jnp.float32

    def cut(values):
        return pl.BlockSpec((block, values.shape[1]), lambda i: (i, 0))

    def whole(values):
        return pl.BlockSpec(values.shape, lambda i: (0, 0))

    results = [
        shape((tokens, width), half),
        shape((tokens, width), full),
        shape((tokens, channels), full),
        shape((tokens, channels), half),
    ]
    sums = [shape((8 + experts, width), full), shape((channels, width), half), shape((width, channels), half)]
    return pl.pallas_call(
        functools.partial(middle_kernel, room),
        grid=(tokens // block,),
        in_specs=[cut(values) for values in blocks] + [whole(values) for values in turned_parts + weights],
        out_specs=[cut(values) for values in results] + [whole(values) for values in sums],
        out_shape=results + sums,
        scratch_shapes=[pltpu.VMEM((tokens, width), half), pltpu.VMEM((tokens, channels), half)],
        compiler_params=pltpu.CompilerParams(vmem_limit_bytes=63 * 1024 * 1024),
        name="middle",
    )(*blocks, *turned_parts, *weights)


def emit_kernel(gi_from, wo_from, wo_other, wi_from, wi_other, in_from, out_from, small_ref, thin_ref,
                gi, w_out, w_in, own_in, own_out, own_x, own_dt, own_taps, own_decay, own_router, *singles):
    gi[...] = gi_from[...]
    w_out[...] = wo_from[...].astype(jnp.float32) + wo_other[...].astype(jnp.float32)
    w_in[...] = wi_from[...].astype(jnp.float32) + wi_other[...].astype(jnp.float32)
    own_in[...] = in_from[...]
    own_out[...] = out_from[...]

    def columns_of(values):
        return jnp.concatenate([values, jnp.zeros((LANES - values.shape[0], LANES), jnp.float32)], axis=0).T

    size, thin = small_ref.shape[0], thin_ref.shape[0]
    first = small_ref[:, :LANES]
    own_x[...] = first[:, : R + 2 * NS]
    own_dt[...] = columns_of(first)[R + 2 * NS :, :size]
    by_row = columns_of(small_ref[:, LANES:])
    own_taps[...] = by_row[:KC, :size]
    own_decay[...] = by_row[8 : 8 + NS, :size]
    for k in range(3):
        singles[k][...] = by_row[24 + k : 25 + k, :size]
    by_row = columns_of(thin_ref[...])
    for k in range(2):
        singles[3 + k][...] = by_row[k : k + 1, :thin]
    own_router[...] = by_row[8 : 8 + own_router.shape[0], :thin]


def emit_outputs(gi, w_out, out_other, w_in, in_other, own_in, own_out, small, thin_part, experts, pieces=4):
    rows, thin = small.shape[0], thin_part.shape[0]
    full = jnp.float32

    def cut(values):
        return pl.BlockSpec((values.shape[0] // pieces, values.shape[1]), lambda i: (i, 0))

    def whole(shape):
        return pl.BlockSpec(shape, lambda i: (0, 0))

    large = [gi, w_out, out_other, w_in, in_other]
    results = [gi, w_out, w_in]
    still = [own_in, own_out, small, thin_part]
    shapes = [own_in.shape, own_out.shape, (rows, R + 2 * NS), (R, rows), (KC, rows), (NS, rows), (experts, thin)]
    shapes += [(1, rows)] * 3 + [(1, thin)] * 2
    return pl.pallas_call(
        emit_kernel,
        grid=(pieces,),
        in_specs=[cut(values) for values in large] + [whole(values.shape) for values in still],
        out_specs=[cut(values) for values in results] + [whole(shape) for shape in shapes],
        out_shape=[jax.ShapeDtypeStruct(values.shape, full) for values in results]
        + [jax.ShapeDtypeStruct(shape, full) for shape in shapes],
        name="emit_outputs",
    )(*large, *still)


def expert_kernel(slices, *refs):
    tokens_ref, grads_ref, column_ref = refs[:3]
    even = range(0, slices, 2)
    odd = range(1, slices, 2)
    weights_in, weight_out = refs[3 : 3 + len(even)], refs[3 + len(even)]
    outs = refs[4 + len(even) :]
    picked_ref, back_ref = outs[:2]
    sums_in = outs[2 : 2 + len(even)]
    kept_out, leaving_out, arriving_out = outs[2 + len(even) : 5 + len(even)]
    (sent, got, answer, returned, w_in, w_out, hidden, total, active, slope, inner, sum_out, pair_out, pair_in, far_out,
     rows_t, send_sems, recv_sems, weight_sems, sum_sems, spread_sems, mate_sems, far_sems, moved_sems) = outs[
        5 + len(even) :
    ]
    experts, room, width = sent.shape[1:]
    places = experts * room
    me = lax.axis_index("exp")
    here = lax.axis_index("ctx")
    levels = slices.bit_length() - 1

    loads = [pltpu.make_async_copy(weight_out, w_out.at[0], weight_sems.at[slices])]
    for k, s in enumerate(even):
        loads.append(pltpu.make_async_copy(weights_in[k], w_in.at[s], weight_sems.at[s]))
    for load in loads:
        load.start()

    barrier = pltpu.get_barrier_semaphore()
    mates = [partner(("ctx", level)) for level in range(levels)]
    for step in range(1, experts):
        pl.semaphore_signal(barrier, inc=1, device_id=(here, lax.rem(me + step, experts)), device_id_type=MESH)
    for mate in mates:
        pl.semaphore_signal(barrier, inc=1, device_id=mate, device_id_type=MESH)
    pl.semaphore_wait(barrier, experts - 1 + levels)

    def exchange(source, target, kind):
        copies = []
        for step in range(1, experts):
            peer = lax.rem(me + step, experts)
            copy = pltpu.make_async_remote_copy(
                src_ref=source.at[peer],
                dst_ref=target.at[me],
                send_sem=send_sems.at[kind, step],
                recv_sem=recv_sems.at[kind, step],
                device_id=(here, peer),
                device_id_type=MESH,
            )
            copy.start()
            copies.append(copy)
        target[me] = source[me]
        return copies

    def hand(source, target, sems, level):
        copy = pltpu.make_async_remote_copy(
            src_ref=source,
            dst_ref=target,
            send_sem=sems.at[0],
            recv_sem=sems.at[1],
            device_id=mates[level],
            device_id_type=MESH,
        )
        copy.start()
        return copy

    def arrive(copies):
        for copy in copies:
            copy.wait_recv()

    open_sends = []

    def spread(level):
        step = 2**level
        copies = [hand(w_out.at[s], w_out.at[s + step], spread_sems.at[1, s + step], level) for s in range(0, slices, 2 * step)]
        open_sends.extend(copies)
        return copies

    spots = lax.broadcasted_iota(jnp.int32, (column_ref.shape[0], places), 1).astype(jnp.float32)
    columns = jnp.concatenate([column_ref[...]] * (places // LANES), axis=1)
    finder = (spots == columns).astype(jnp.float32).astype(jnp.bfloat16)
    sent[0] = contract(finder, tokens_ref[...], 0, 0).astype(jnp.bfloat16).reshape(experts, room, width)
    first = exchange(sent.at[0], got.at[0], 0)
    for load in loads:
        load.wait()
    widening = [spread(levels - 1)]
    paired = [hand(w_in.at[s], w_in.at[s + 1], spread_sems.at[0, s], 0) for s in even]
    sent[1] = contract(finder, grads_ref[...], 0, 0).astype(jnp.bfloat16).reshape(experts, room, width)
    second = exchange(sent.at[1], got.at[1], 1)

    arrive(first)
    rows = got[0].reshape(places, width)
    for s in list(even) + list(odd):
        if s == 1:
            arrive(paired)
        hidden[...] = dot(rows, w_in[s])

        def curve(index, unused):
            at = pl.ds(pl.multiple_of(index * ROWS_AT_ONCE, ROWS_AT_ONCE), ROWS_AT_ONCE)
            value = hidden[at, :]
            bell = 0.5 + 0.5 * lax.erf(value * 0.7071067811865476)
            active[s, at, :] = (value * bell).astype(jnp.bfloat16)
            slope[s, at, :] = bell + value * (jnp.exp(-0.5 * value * value) * 0.3989422804014327)
            return unused

        lax.fori_loop(0, places // ROWS_AT_ONCE, curve, 0)

    for level in reversed(range(levels - 1)):
        arrive(widening[-1])
        widening.append(spread(level))
    for s in list(even) + list(odd):
        if s == 1:
            arrive(widening[-1])
        product = dot(active[s], w_out[s])
        total[...] = product if s == 0 else total[...] + product
    answer[0] = total[...].astype(jnp.bfloat16).reshape(experts, room, width)
    third = exchange(answer.at[0], returned.at[0], 2)

    arrive(second)
    pulled = got[1].reshape(places, width)
    for s in range(slices):
        inner[s] = (contract(pulled, w_out[s], 1, 1) * slope[s]).astype(jnp.bfloat16)
        product = contract(inner[s], w_in[s], 1, 1)
        total[...] = product if s == 0 else total[...] + product
    answer[1] = total[...].astype(jnp.bfloat16).reshape(experts, room, width)
    fourth = exchange(answer.at[1], returned.at[1], 3)
    joining = []
    for s in list(odd) + list(even):
        sum_out[s] = contract(active[s], pulled, 0, 0).astype(jnp.bfloat16)
        if s % 2:
            joining.append(hand(sum_out.at[s], pair_out.at[s // 2], mate_sems.at[0, s // 2], 0))

    def add_into(target, addend):
        def some(index, unused):
            at = pl.ds(pl.multiple_of(index * 4 * ROWS_AT_ONCE, 4 * ROWS_AT_ONCE), 4 * ROWS_AT_ONCE)
            target[at, :] = target[at, :] + addend[at, :]
            return unused

        lax.fori_loop(0, target.shape[0] // (4 * ROWS_AT_ONCE), some, 0)

    arrive(joining)
    for k, s in enumerate(even):
        add_into(sum_out.at[s], pair_out.at[k])

    def pass_on(level):
        step = 2**level
        return [
            hand(sum_out.at[s + step], far_out.at[slices // step // 2 - 1 + s // (2 * step)], far_sems.at[level, s // (2 * step)], level)
            for s in range(0, slices, 2 * step)
        ]

    open_sends.extend(joining)
    for level in range(1, levels - 1):
        passing = pass_on(level)
        arrive(passing)
        open_sends.extend(passing)
        step = 2**level
        for s in range(0, slices, 2 * step):
            add_into(sum_out.at[s], far_out.at[slices // step // 2 - 1 + s // (2 * step)])
    stores = [
        pltpu.make_async_copy(sum_out.at[0], kept_out, sum_sems.at[len(even)]),
        pltpu.make_async_copy(sum_out.at[slices // 2], leaving_out, sum_sems.at[len(even) + 1]),
    ]
    for store in stores:
        store.start()
    move = row_half(sum_out.at[slices // 2], arriving_out, moved_sems, ("ctx", levels - 1), 0)
    move.start()
    for low in range(0, places, LANES):
        for left in range(0, width, LANES):
            square = got[0].reshape(places, width)[low : low + LANES, left : left + LANES].astype(jnp.float32).T
            rows_t[left : left + LANES, low : low + LANES] = square.astype(jnp.bfloat16)
    for copy in paired:
        copy.wait_send()
    joined = []
    for s in list(odd) + list(even):
        w_in[s] = dot(rows_t[...], inner[s]).astype(jnp.bfloat16)
        if s % 2:
            joined.append(hand(w_in.at[s], pair_in.at[s // 2], mate_sems.at[1, s // 2], 0))
    arrive(joined)
    for k, s in enumerate(even):
        add_into(w_in.at[s], pair_in.at[k])
        stores.append(pltpu.make_async_copy(w_in.at[s], sums_in[k], sum_sems.at[k]))
        stores[-1].start()

    arrive(third)
    picked_ref[...] = dot(finder, returned[0].reshape(places, width)).astype(jnp.bfloat16)
    arrive(fourth)
    back_ref[...] = dot(finder, returned[1].reshape(places, width)).astype(jnp.bfloat16)
    for store in stores:
        store.wait()
    move.wait()
    for copies in (first, second, third, fourth, joined, open_sends):
        for copy in copies:
            copy.wait_send()


def run_experts(rows, grads, target, weights_in, weight_out, experts, room, identity):
    slices = 2 * len(weights_in)
    tokens, width = rows.shape
    inner_width = weight_out.shape[0]
    places = experts * room
    inside = pl.BlockSpec(memory_space=pltpu.VMEM)
    anywhere = pl.BlockSpec(memory_space=pl.ANY)
    half = jnp.bfloat16
    count = len(weights_in)
    out = pl.pallas_call(
        functools.partial(expert_kernel, slices),
        in_specs=[inside] * 3 + [anywhere] * (count + 1),
        out_specs=[inside] * 2 + [anywhere] * (count + 3),
        out_shape=[jax.ShapeDtypeStruct(rows.shape, half)] * 2
        + [jax.ShapeDtypeStruct(weight.shape, half) for weight in weights_in]
        + [jax.ShapeDtypeStruct(weight_out.shape, half)] * 3,
        scratch_shapes=[pltpu.VMEM((2, experts, room, width), half)] * 4
        + [
            pltpu.VMEM((slices, width, inner_width), half),
            pltpu.VMEM((slices, inner_width, width), half),
            pltpu.VMEM((places, inner_width), jnp.float32),
            pltpu.VMEM((places, width), jnp.float32),
            pltpu.VMEM((slices, places, inner_width), half),
            pltpu.VMEM((slices, places, inner_width), jnp.float32),
            pltpu.VMEM((slices, places, inner_width), half),
            pltpu.VMEM((slices, inner_width, width), half),
            pltpu.VMEM((count, inner_width, width), half),
            pltpu.VMEM((count, width, inner_width), half),
            pltpu.VMEM((count, inner_width, width), half),
            pltpu.VMEM((width, places), half),
            pltpu.SemaphoreType.DMA((4, experts)),
            pltpu.SemaphoreType.DMA((4, experts)),
            pltpu.SemaphoreType.DMA((slices + 1,)),
            pltpu.SemaphoreType.DMA((count + 2,)),
            pltpu.SemaphoreType.DMA((2, slices, 2)),
            pltpu.SemaphoreType.DMA((2, count, 2)),
            pltpu.SemaphoreType.DMA((slices, count, 2)),
            pltpu.SemaphoreType.DMA((2, 2)),
        ],
        compiler_params=pltpu.CompilerParams(
            collective_id=identity, has_side_effects=True, vmem_limit_bytes=63 * 1024 * 1024
        ),
        name="run_experts",
    )(rows, grads, target, *weights_in, weight_out)
    return out[0], out[1], list(out[2 : 2 + count]), out[2 + count :]


def flipped(value, level):
    count = lax.axis_size("ctx")
    return lax.ppermute(value, "ctx", [(source, source ^ (1 << level)) for source in range(count)])


def spread_slices(own, far):
    levels = lax.axis_size("ctx").bit_length() - 1
    slices = {0: own, 1 << (levels - 1): far}
    for level in reversed(range(1, levels - 1)):
        for offset in sorted(slices):
            slices[offset + (1 << level)] = flipped(slices[offset], level)
    return [slices[offset] for offset in sorted(slices)]


def collect_slices(sums):
    levels = lax.axis_size("ctx").bit_length() - 1
    for level in range(1, levels - 1):
        arrived = [flipped(values, level).astype(jnp.float32) for values in sums[1::2]]
        sums = [
            (values.astype(jnp.float32) + other).astype(jnp.bfloat16) for values, other in zip(sums[::2], arrived)
        ]
    return sums


def body(
    inputs,
    segments,
    routes,
    cotangent,
    norm_gain,
    in_proj,
    conv_taps,
    conv_bias,
    x_proj,
    dt_proj,
    dt_bias,
    log_decay,
    skip_gain,
    out_proj,
    moe_gain,
    router,
    expert_in,
    expert_out,
):
    experts = router.shape[1]
    half_rows = norm_gain.shape[0]
    small = (
        x_proj,
        dt_proj,
        conv_taps.T,
        log_decay.T,
        jnp.stack([conv_bias, dt_bias, skip_gain]),
        jnp.stack([norm_gain, moe_gain]),
        router.T,
    )
    sizes = [(name, lax.axis_size(name)) for name in ("ctx", "exp")]
    weights, partial, begun, *prior = gather_all(
        sizes, small, in_proj, out_proj, inputs[0], segments, expert_in[0], 0
    )
    tokens_here = inputs.shape[1]
    capacity = 5 * tokens_here // (4 * experts)
    room = -(-capacity // 16) * 16
    (
        scan_rows,
        products,
        normed_one,
        b_turned,
        c_turned,
        rates,
        by_channel,
        gain_rows,
        delta_low,
        same_rows,
        target,
        kept,
        (conv_ext, conv_out, xs_val, dt_pre, masked_step, push),
        (full_gate, full_out),
        far_in,
    ) = scan_forward(
        sizes,
        inputs[0],
        prior,
        (segments, routes.reshape(1, tokens_here)),
        weights,
        room,
        partial,
        expert_in[0],
        begun,
        3,
    )
    weights_in = spread_slices(expert_in[0], far_in)
    full_conv, full_channel, full_width = weights
    normed_two, residual, gate_z, probability, grad_pick, gated_turned, normed_turned = open_gate(
        scan_rows,
        xs_val,
        normed_one,
        inputs[0],
        cotangent[0],
        target,
        [full_gate, full_out, full_width, by_channel, gain_rows],
        room,
        experts,
    )
    picked, grad_from_experts, grad_expert_in, (kept_out, leaving_out, begun_out) = run_experts(
        normed_two, grad_pick, target, weights_in, expert_out[0], experts, room, 2
    )
    kept_in, leaving = collect_slices(grad_expert_in)
    out_block, grad_resid, grad_y, grad_z, wide_rows, grad_out_proj, grad_gate_proj = middle(
        [picked, grad_from_experts, cotangent[0], residual, gate_z, scan_rows, xs_val, normed_two, probability, target],
        [gated_turned, normed_turned],
        [full_out, full_width, by_channel, gain_rows],
        room,
        experts,
    )
    along_b, slope, grad_bs, grad_cs, grad_a, partial_sums, begun_in = scan_backward(
        sizes,
        masked_step,
        push,
        grad_y,
        b_turned,
        c_turned,
        rates,
        products,
        (grad_gate_proj, grad_out_proj),
        kept,
        leaving,
        4,
    )
    finished = finish(
        sizes,
        (along_b, slope, grad_y, dt_pre, conv_out, xs_val, conv_ext, grad_z, full_conv, full_gate),
        (
            normed_turned,
            inputs[0],
            grad_resid,
            full_channel,
            jnp.pad(jnp.concatenate([grad_bs, grad_cs], axis=1), ((0, 0), (R, LANES - R - 2 * NS))),
            delta_low,
            same_rows,
            by_channel,
            grad_a,
            rates,
            wide_rows,
        ),
        partial_sums,
        (leaving, leaving_out),
        (begun_in, begun_out),
        1,
    )
    grad_inputs, own_in, own_out, own_small, own_thin, arrived, arrived_out = finished
    grad_inputs, grad_w_out, grad_w_in, own_in, own_out, own_x, own_dt, own_taps, own_decay, own_router, *vectors = (
        emit_outputs(
            grad_inputs, kept_out, arrived_out, kept_in, arrived, own_in, own_out, own_small, own_thin, experts
        )
    )
    own_bias, own_dtbias, own_skip, own_norm, own_moe = [values[0] for values in vectors]
    return (
        out_block[None],
        grad_inputs[None],
        own_norm,
        own_in,
        own_taps.T,
        own_bias,
        own_x,
        own_dt,
        own_dtbias,
        own_decay.T,
        own_skip,
        own_out,
        own_moe,
        own_router.T,
        grad_w_in[None],
        grad_w_out[None],
    )


def solution(mesh):
    placed = (
        P("exp", "ctx", None),
        P("exp", "ctx"),
        P("exp", "ctx", None),
        P("exp", "ctx", None),
        P(("ctx", "exp")),
        P(("ctx", "exp"), None),
        P(("ctx", "exp"), None),
        P(("ctx", "exp")),
        P(("ctx", "exp"), None),
        P(None, ("ctx", "exp")),
        P(("ctx", "exp")),
        P(("ctx", "exp"), None),
        P(("ctx", "exp")),
        P(("ctx", "exp"), None),
        P(("ctx", "exp")),
        P(("ctx", "exp"), None),
        P("exp", None, "ctx"),
        P("exp", "ctx", None),
    )
    return jax.shard_map(
        body,
        mesh=mesh,
        in_specs=placed,
        out_specs=(
            P("exp", "ctx", None),
            P("exp", "ctx", None),
            P(("ctx", "exp")),
            P(("ctx", "exp"), None),
            P(("ctx", "exp"), None),
            P(("ctx", "exp")),
            P(("ctx", "exp"), None),
            P(None, ("ctx", "exp")),
            P(("ctx", "exp")),
            P(("ctx", "exp"), None),
            P(("ctx", "exp")),
            P(("ctx", "exp"), None),
            P(("ctx", "exp")),
            P(("ctx", "exp"), None),
            P("exp", None, "ctx"),
            P("exp", "ctx", None),
        ),
        check_vma=False,
    )
```

profile of v0, /device:TPU:0, one launch (start us, length us, event | category | flops | bytes accessed | tf_op | source)
XLA Modules:
  0.0 312.6 jit_solution(12132009572450254100)
XLA Ops:
  0.6 1.2 pad_maximum_fusion.1.refs_5_
  1.8 1.3 pad_maximum_fusion.refs_4_
  3.1 36.0 %gather_all.1 = (bf16[2,2,2,2,2,24,1536]{6,5,4,3,2,1,0:T(8,128)(2,1)}, bf16[2,2,2,2,2,48,256]{6,5,4,3,2,1,0:T(8,128)(2,1)}, bf16[2,2,2,2,2,24,128]{6,5,4,3,2,1,0...) custom-call(bf16[48,80]{1,0:T(8,128)(2,1)} %refs_0_.1, ...), custom_call_target="tpu_custom_call" | custom-call | tf_op jit(solution)/shard_map/gather_all/pallas_call | solution.py:240
  39.1 49.9 %scan_forward.1 = (f32[384,1536]{1,0:T(8,128)}, bf16[4,16,1536]{2,1,0:T(8,128)(2,1)}, bf16[384,768]{1,0:T(8,128)(2,1)}, f32[16,384]{1,0:T(8,128)}, f32[16,384]{1...) custom-call(bf16[384,768]{1,0:T(8,128)(2,1)} %bitcast.37, ...), custom_call_target="tpu_custom_call", output_to_operand_aliasing={{20}: (11, {})} | custom-call | flops 84934656 | bytes 84934656 | tf_op jit(solution)/shard_map/scan_forward/pallas_call | solution.py:819
  89.0 9.7 %open_gate.1 = (bf16[384,768]{1,0:T(8,128)(2,1)}, f32[384,768]{1,0:T(8,128)}, f32[384,1536]{1,0:T(8,128)}, f32[384,128]{1,0:T(8,128)}, bf16[384,768]{1,0:T(8,128...) custom-call(f32[384,1536]{1,0:T(8,128)} %get-tuple-element.104.y_ref, ...), custom_call_target="tpu_custom_call" | custom-call | tf_op jit(solution)/shard_map/open_gate/pallas_call | solution.py:1391
  98.6 70.7 %run_experts.1 = (bf16[384,768]{1,0:T(8,128)(2,1)}, bf16[384,768]{1,0:T(8,128)(2,1)}, bf16[768,768]{1,0:T(8,128)(2,1)}, bf16[768,768]{1,0:T(8,128)(2,1)}, bf16[7...) custom-call(bf16[384,768]{1,0:T(8,128)(2,1)} %get-tuple-element.112.refs_0_.n2_ref, ...), custom_call_target="tpu_custom_call" | custom-call | tf_op jit(solution)/shard_map/run_experts/pallas_call | solution.py:1744
  169.3 15.4 %middle.1 = (bf16[384,768]{1,0:T(8,128)(2,1)}, f32[384,768]{1,0:T(8,128)}, f32[384,1536]{1,0:T(8,128)}, bf16[384,1536]{1,0:T(8,128)(2,1)}, f32[16,768]{1,0:T(8,1...) custom-call(bf16[384,768]{1,0:T(8,128)(2,1)} %get-tuple-element.115.picked_ref, ...), custom_call_target="tpu_custom_call" | custom-call | tf_op jit(solution)/shard_map/middle/pallas_call | solution.py:1479
  184.7 63.9 %scan_backward.1 = (f32[6,8,1024]{2,1,0:T(8,128)}, f32[6,8,1024]{2,1,0:T(8,128)}, f32[16,1536]{1,0:T(8,128)}, bf16[2,2,24,1536]{3,2,1,0:T(8,128)(2,1)}, bf16[2,2...) custom-call(f32[16,384]{1,0:T(8,128)} %get-tuple-element.123.refs_0_, ...), custom_call_target="tpu_custom_call" | custom-call | flops 141557760 | bytes 141557760 | tf_op jit(solution)/shard_map/scan_backward/pallas_call | solution.py:977
  248.6 1.1 slice_reduce_fusion
  249.7 0.1 reshape_squeeze.7
  249.9 0.1 reshape_squeeze.6
  250.0 0.9 select_maximum_fusion.refs_14_
  250.8 55.5 %finish.1 = (f32[384,768]{1,0:T(8,128)}, f32[24,3072]{1,0:T(8,128)}, f32[48,768]{1,0:T(8,128)}, f32[48,256]{1,0:T(8,128)}, f32[24,128]{1,0:T(8,128)}, /*index=5*...) custom-call(f32[384,1536]{1,0:T(8,128)} %get-tuple-element.134.refs_0_, ...), custom_call_target="tpu_custom_call", output_to_operand_aliasing={{5}: (25, {}), {6}: (26, {})} | custom-call | tf_op jit(solution)/shard_map/finish/pallas_call | solution.py:1297
  306.4 6.0 %emit_outputs.1 = (f32[384,768]{1,0:T(8,128)}, f32[768,768]{1,0:T(8,128)}, f32[768,768]{1,0:T(8,128)}, f32[24,3072]{1,0:T(8,128)}, f32[48,768]{1,0:T(8,128)}, /*...) custom-call(f32[384,768]{1,0:T(8,128)} %get-tuple-element.152.gi_fro, ...), custom_call_target="tpu_custom_call" | custom-call | tf_op jit(solution)/shard_map/emit_outputs/pallas_call | solution.py:1532
where the time goes:
time: 315 us; the launch traced here: 313 us
  Pallas kernels  307 us (97%)
  other arithmetic  3.3 us (1%)
    pallas_call x1, Pallas kernels, run_experts(): pl.pallas_call(functools.partial(expert_kernel, slices), in_specs=[inside...  70.7 us
    pallas_call x1, Pallas kernels, scan_backward(): pl.pallas_call(functools.partial(backward_kernel, places, streams, len(la...  63.9 us
    pallas_call x1, Pallas kernels, finish(): pl.pallas_call(functools.partial(finish_kernel, places, streams, third, l...  55.5 us
    pallas_call x1, Pallas kernels, scan_forward(): pl.pallas_call(functools.partial(forward_kernel, places, streams, pick(ch...  49.9 us
    pallas_call x1, Pallas kernels, gather_all(): pl.pallas_call(functools.partial(gather_kernel, places, streams, late, fa...  36 us
    pallas_call x1, Pallas kernels, middle(): pl.pallas_call(functools.partial(middle_kernel, room), grid=(tokens // bl...  15.4 us
    pallas_call x1, Pallas kernels, open_gate(): pl.pallas_call(functools.partial(gate_kernel, room, experts), grid=(token...  9.65 us

commit v1 on v0

--- a/solution.py
+++ b/solution.py
@@ -53,11 +53,16 @@
     return (where["ctx"], where["exp"])
 
 
-def meet(places, *others):
+def greet(places, *others):
     barrier = pltpu.get_barrier_semaphore()
     for device in [partner(place) for place in places] + list(others):
         pl.semaphore_signal(barrier, inc=1, device_id=device, device_id_type=MESH)
-    pl.semaphore_wait(barrier, len(places) + len(others))
+    return len(places) + len(others)
+
+
+def meet(places, *others):
+    count = greet(places, *others)
+    pl.semaphore_wait(pltpu.get_barrier_semaphore(), count)
 
 
 class GatherFlow:
@@ -144,7 +149,6 @@
      edge_sems, moved_sems) = refs[20:]
     split = in_ref.shape[1] // 2
     shards = (in_ref.at[:, :split], channel_pack, width_pack, in_ref.at[:, split:], out_ref)
-    pack_small(small, square, channel_pack, width_pack)
     count = 3
     flow = GatherFlow(
         places, streams, range(len(places)), shards[:count], wholes[:count], send_sems, recv_sems, local_sems
@@ -154,7 +158,9 @@
     )
     blocks = lax.axis_size("ctx")
     here, line = lax.axis_index("ctx"), lax.axis_index("exp")
-    meet(places, (lax.rem(here + 1, blocks), line), (lax.rem(here + blocks - 1, blocks), line))
+    count_met = greet(places, (lax.rem(here + 1, blocks), line), (lax.rem(here + blocks - 1, blocks), line))
+    pack_small(small, square, channel_pack, width_pack)
+    pl.semaphore_wait(pltpu.get_barrier_semaphore(), count_met)
     flow.start()
     tokens = rows_ref.shape[0]
     edges = [
@@ -921,11 +927,12 @@
     flow.start()
     move = row_half(leaving, arriving, moved_sems, ("ctx", blocks.bit_length() - 2), 0)
     move.start()
-    spread_columns(bt_ref, wide_b)
     spread_columns(ct_ref, wide_c)
     inflow_pass(width, step_ref, grad_ref, wide_c, rate_ref, flow_ref, ready)
     message[...] = flow_ref[...].astype(jnp.bfloat16)
     copies = share(message, inflows, share_sems.at[0], share_sems.at[1])
+    flow.advance(0)
+    spread_columns(bt_ref, wide_b)
     for copy in copies:
         copy.wait_recv()
     end = jnp.zeros(flow_ref.shape, jnp.float32)
@@ -933,18 +940,17 @@
         folded = inflows[index].astype(jnp.float32) + product_ref[index].astype(jnp.float32) * end
         end = jnp.where(index > position, folded, end)
     flow_ref[...] = end
-    flow.advance(0)
     push_load.wait()
 
     def hook(order):
         for k in range(2):
             rows_copy(steps - 1 - order, k).start()
 
-        @pl.when(order == 2)
+        @pl.when(order == 3)
         def _():
             flow.advance(1)
 
-        @pl.when(order == 4)
+        @pl.when(order == 5)
         def _():
             flow.advance(2)
 
@@ -1458,7 +1464,7 @@
         lax.fori_loop(0, sum_gate.shape[1] // piece, other, 0)
 
 
-def middle(blocks, turned_parts, weights, room, experts, block=3 * LANES):
+def middle(blocks, turned_parts, weights, room, experts, block=192):
     tokens, width = blocks[0].shape
     channels = turned_parts[0].shape[0]
     shape, half, full = jax.ShapeDtypeStruct, jnp.bfloat16, jnp.float32
@@ -1514,7 +1520,7 @@
     own_router[...] = by_row[8 : 8 + own_router.shape[0], :thin]
 
 
-def emit_outputs(gi, w_out, out_other, w_in, in_other, own_in, own_out, small, thin_part, experts, pieces=4):
+def emit_outputs(gi, w_out, out_other, w_in, in_other, own_in, own_out, small, thin_part, experts, pieces=2):
     rows, thin = small.shape[0], thin_part.shape[0]
     full = jnp.float32
 
@@ -1571,7 +1577,6 @@
         pl.semaphore_signal(barrier, inc=1, device_id=(here, lax.rem(me + step, experts)), device_id_type=MESH)
     for mate in mates:
         pl.semaphore_signal(barrier, inc=1, device_id=mate, device_id_type=MESH)
-    pl.semaphore_wait(barrier, experts - 1 + levels)
 
     def exchange(source, target, kind):
         copies = []
@@ -1618,6 +1623,7 @@
     columns = jnp.concatenate([column_ref[...]] * (places // LANES), axis=1)
     finder = (spots == columns).astype(jnp.float32).astype(jnp.bfloat16)
     sent[0] = contract(finder, tokens_ref[...], 0, 0).astype(jnp.bfloat16).reshape(experts, room, width)
+    pl.semaphore_wait(barrier, experts - 1 + levels)
     first = exchange(sent.at[0], got.at[0], 0)
     for load in loads:
         load.wait()

time: 315 us -> 311 us (0.987)
  Pallas kernels: 307 us -> 303 us
where the time goes in v1:
time: 311 us; the launch traced here: 309 us
  Pallas kernels  303 us (97%)
  other arithmetic  3.3 us (1%)
    pallas_call x1, Pallas kernels, run_experts(): pl.pallas_call(functools.partial(expert_kernel, slices), in_specs=[inside...  69.9 us
    pallas_call x1, Pallas kernels, scan_backward(): pl.pallas_call(functools.partial(backward_kernel, places, streams, len(la...  61.2 us
    pallas_call x1, Pallas kernels, finish(): pl.pallas_call(functools.partial(finish_kernel, places, streams, third, l...  56.4 us
    pallas_call x1, Pallas kernels, scan_forward(): pl.pallas_call(functools.partial(forward_kernel, places, streams, pick(ch...  49.9 us
    pallas_call x1, Pallas kernels, gather_all(): pl.pallas_call(functools.partial(gather_kernel, places, streams, late, fa...  35.8 us
    pallas_call x1, Pallas kernels, middle(): pl.pallas_call(functools.partial(middle_kernel, room), grid=(tokens // bl...  15 us
    pallas_call x1, Pallas kernels, open_gate(): pl.pallas_call(functools.partial(gate_kernel, room, experts), grid=(token...  9.65 us

profile of v1, /device:TPU:0, one launch (start us, length us, event | category | flops | bytes accessed | tf_op | source)
XLA Modules:
  0.0 308.6 jit_solution(1430695133613871586)
XLA Ops:
  0.6 1.2 pad_maximum_fusion.1.refs_5_
  1.8 1.3 pad_maximum_fusion.refs_4_
  3.1 35.8 %gather_all.1 = (bf16[2,2,2,2,2,24,1536]{6,5,4,3,2,1,0:T(8,128)(2,1)}, bf16[2,2,2,2,2,48,256]{6,5,4,3,2,1,0:T(8,128)(2,1)}, bf16[2,2,2,2,2,24,128]{6,5,4,3,2,1,0...) custom-call(bf16[48,80]{1,0:T(8,128)(2,1)} %refs_0_.1, ...), custom_call_target="tpu_custom_call" | custom-call | tf_op jit(solution)/shard_map/gather_all/pallas_call | solution.py:246
  38.9 49.9 %scan_forward.1 = (f32[384,1536]{1,0:T(8,128)}, bf16[4,16,1536]{2,1,0:T(8,128)(2,1)}, bf16[384,768]{1,0:T(8,128)(2,1)}, f32[16,384]{1,0:T(8,128)}, f32[16,384]{1...) custom-call(bf16[384,768]{1,0:T(8,128)(2,1)} %bitcast.37, ...), custom_call_target="tpu_custom_call", output_to_operand_aliasing={{20}: (11, {})} | custom-call | flops 84934656 | bytes 84934656 | tf_op jit(solution)/shard_map/scan_forward/pallas_call | solution.py:825
  88.8 9.7 %open_gate.1 = (bf16[384,768]{1,0:T(8,128)(2,1)}, f32[384,768]{1,0:T(8,128)}, f32[384,1536]{1,0:T(8,128)}, f32[384,128]{1,0:T(8,128)}, bf16[384,768]{1,0:T(8,128...) custom-call(f32[384,1536]{1,0:T(8,128)} %get-tuple-element.104.y_ref, ...), custom_call_target="tpu_custom_call" | custom-call | tf_op jit(solution)/shard_map/open_gate/pallas_call | solution.py:1397
  98.4 69.9 %run_experts.1 = (bf16[384,768]{1,0:T(8,128)(2,1)}, bf16[384,768]{1,0:T(8,128)(2,1)}, bf16[768,768]{1,0:T(8,128)(2,1)}, bf16[768,768]{1,0:T(8,128)(2,1)}, bf16[7...) custom-call(bf16[384,768]{1,0:T(8,128)(2,1)} %get-tuple-element.112.refs_0_.n2_ref, ...), custom_call_target="tpu_custom_call" | custom-call | tf_op jit(solution)/shard_map/run_experts/pallas_call | solution.py:1750
  168.3 15.0 %middle.1 = (bf16[384,768]{1,0:T(8,128)(2,1)}, f32[384,768]{1,0:T(8,128)}, f32[384,1536]{1,0:T(8,128)}, bf16[384,1536]{1,0:T(8,128)(2,1)}, f32[16,768]{1,0:T(8,1...) custom-call(bf16[384,768]{1,0:T(8,128)(2,1)} %get-tuple-element.115.picked_ref, ...), custom_call_target="tpu_custom_call" | custom-call | tf_op jit(solution)/shard_map/middle/pallas_call | solution.py:1485
  183.3 61.2 %scan_backward.1 = (f32[6,8,1024]{2,1,0:T(8,128)}, f32[6,8,1024]{2,1,0:T(8,128)}, f32[16,1536]{1,0:T(8,128)}, bf16[2,2,24,1536]{3,2,1,0:T(8,128)(2,1)}, bf16[2,2...) custom-call(f32[16,384]{1,0:T(8,128)} %get-tuple-element.123.refs_0_, ...), custom_call_target="tpu_custom_call" | custom-call | flops 141557760 | bytes 141557760 | tf_op jit(solution)/shard_map/scan_backward/pallas_call | solution.py:983
  244.5 1.1 slice_reduce_fusion
  245.7 0.1 reshape_squeeze.7
  245.8 0.1 reshape_squeeze.6
  245.9 0.9 select_maximum_fusion.refs_14_
  246.8 56.4 %finish.1 = (f32[384,768]{1,0:T(8,128)}, f32[24,3072]{1,0:T(8,128)}, f32[48,768]{1,0:T(8,128)}, f32[48,256]{1,0:T(8,128)}, f32[24,128]{1,0:T(8,128)}, /*index=5*...) custom-call(f32[384,1536]{1,0:T(8,128)} %get-tuple-element.134.refs_0_, ...), custom_call_target="tpu_custom_call", output_to_operand_aliasing={{5}: (25, {}), {6}: (26, {})} | custom-call | tf_op jit(solution)/shard_map/finish/pallas_call | solution.py:1303
  303.1 5.3 %emit_outputs.1 = (f32[384,768]{1,0:T(8,128)}, f32[768,768]{1,0:T(8,128)}, f32[768,768]{1,0:T(8,128)}, f32[24,3072]{1,0:T(8,128)}, f32[48,768]{1,0:T(8,128)}, /*...) custom-call(f32[384,768]{1,0:T(8,128)} %get-tuple-element.152.gi_fro, ...), custom_call_target="tpu_custom_call" | custom-call | tf_op jit(solution)/shard_map/emit_outputs/pallas_call | solution.py:1538

commit v2 on v1

--- a/solution.py
+++ b/solution.py
@@ -786,7 +786,7 @@
         )
 
     def hook(number):
-        @pl.when(number == 3)
+        @pl.when(number == 4)
         def _():
             flow.advance(1)
 

time: 311 us -> 309 us (level)
  no operation moved by 1% of the time
where the time goes in v2:
time: 309 us; the launch traced here: 306 us
  Pallas kernels  301 us (97%)
  other arithmetic  3.3 us (1%)
    pallas_call x1, Pallas kernels, run_experts(): pl.pallas_call(functools.partial(expert_kernel, slices), in_specs=[inside...  70.3 us
    pallas_call x1, Pallas kernels, scan_backward(): pl.pallas_call(functools.partial(backward_kernel, places, streams, len(la...  61.2 us
    pallas_call x1, Pallas kernels, finish(): pl.pallas_call(functools.partial(finish_kernel, places, streams, third, l...  55 us
    pallas_call x1, Pallas kernels, scan_forward(): pl.pallas_call(functools.partial(forward_kernel, places, streams, pick(ch...  48.5 us
    pallas_call x1, Pallas kernels, gather_all(): pl.pallas_call(functools.partial(gather_kernel, places, streams, late, fa...  35.8 us
    pallas_call x1, Pallas kernels, middle(): pl.pallas_call(functools.partial(middle_kernel, room), grid=(tokens // bl...  15 us
    pallas_call x1, Pallas kernels, open_gate(): pl.pallas_call(functools.partial(gate_kernel, room, experts), grid=(token...  9.65 us

profile of v2, /device:TPU:0, one launch (start us, length us, event | category | flops | bytes accessed | tf_op | source)
XLA Modules:
  0.0 306.3 jit_solution(7257776064414074094)
XLA Ops:
  0.6 1.2 pad_maximum_fusion.1.refs_5_
  1.8 1.3 pad_maximum_fusion.refs_4_
  3.1 35.8 %gather_all.1 = (bf16[2,2,2,2,2,24,1536]{6,5,4,3,2,1,0:T(8,128)(2,1)}, bf16[2,2,2,2,2,48,256]{6,5,4,3,2,1,0:T(8,128)(2,1)}, bf16[2,2,2,2,2,24,128]{6,5,4,3,2,1,0...) custom-call(bf16[48,80]{1,0:T(8,128)(2,1)} %refs_0_.1, ...), custom_call_target="tpu_custom_call" | custom-call | tf_op jit(solution)/shard_map/gather_all/pallas_call | solution.py:246
  38.9 48.5 %scan_forward.1 = (f32[384,1536]{1,0:T(8,128)}, bf16[4,16,1536]{2,1,0:T(8,128)(2,1)}, bf16[384,768]{1,0:T(8,128)(2,1)}, f32[16,384]{1,0:T(8,128)}, f32[16,384]{1...) custom-call(bf16[384,768]{1,0:T(8,128)(2,1)} %bitcast.37, ...), custom_call_target="tpu_custom_call", output_to_operand_aliasing={{20}: (11, {})} | custom-call | flops 84934656 | bytes 84934656 | tf_op jit(solution)/shard_map/scan_forward/pallas_call | solution.py:825
  87.4 9.6 %open_gate.1 = (bf16[384,768]{1,0:T(8,128)(2,1)}, f32[384,768]{1,0:T(8,128)}, f32[384,1536]{1,0:T(8,128)}, f32[384,128]{1,0:T(8,128)}, bf16[384,768]{1,0:T(8,128...) custom-call(f32[384,1536]{1,0:T(8,128)} %get-tuple-element.104.y_ref, ...), custom_call_target="tpu_custom_call" | custom-call | tf_op jit(solution)/shard_map/open_gate/pallas_call | solution.py:1397
  97.1 70.3 %run_experts.1 = (bf16[384,768]{1,0:T(8,128)(2,1)}, bf16[384,768]{1,0:T(8,128)(2,1)}, bf16[768,768]{1,0:T(8,128)(2,1)}, bf16[768,768]{1,0:T(8,128)(2,1)}, bf16[7...) custom-call(bf16[384,768]{1,0:T(8,128)(2,1)} %get-tuple-element.112.refs_0_.n2_ref, ...), custom_call_target="tpu_custom_call" | custom-call | tf_op jit(solution)/shard_map/run_experts/pallas_call | solution.py:1750
  167.4 15.0 %middle.1 = (bf16[384,768]{1,0:T(8,128)(2,1)}, f32[384,768]{1,0:T(8,128)}, f32[384,1536]{1,0:T(8,128)}, bf16[384,1536]{1,0:T(8,128)(2,1)}, f32[16,768]{1,0:T(8,1...) custom-call(bf16[384,768]{1,0:T(8,128)(2,1)} %get-tuple-element.115.picked_ref, ...), custom_call_target="tpu_custom_call" | custom-call | tf_op jit(solution)/shard_map/middle/pallas_call | solution.py:1485
  182.4 61.2 %scan_backward.1 = (f32[6,8,1024]{2,1,0:T(8,128)}, f32[6,8,1024]{2,1,0:T(8,128)}, f32[16,1536]{1,0:T(8,128)}, bf16[2,2,24,1536]{3,2,1,0:T(8,128)(2,1)}, bf16[2,2...) custom-call(f32[16,384]{1,0:T(8,128)} %get-tuple-element.123.refs_0_, ...), custom_call_target="tpu_custom_call" | custom-call | flops 141557760 | bytes 141557760 | tf_op jit(solution)/shard_map/scan_backward/pallas_call | solution.py:983
  243.6 1.1 slice_reduce_fusion
  244.8 0.1 reshape_squeeze.7
  244.9 0.1 reshape_squeeze.6
  245.0 0.9 select_maximum_fusion.refs_14_
  245.9 55.0 %finish.1 = (f32[384,768]{1,0:T(8,128)}, f32[24,3072]{1,0:T(8,128)}, f32[48,768]{1,0:T(8,128)}, f32[48,256]{1,0:T(8,128)}, f32[24,128]{1,0:T(8,128)}, /*index=5*...) custom-call(f32[384,1536]{1,0:T(8,128)} %get-tuple-element.134.refs_0_, ...), custom_call_target="tpu_custom_call", output_to_operand_aliasing={{5}: (25, {}), {6}: (26, {})} | custom-call | tf_op jit(solution)/shard_map/finish/pallas_call | solution.py:1303
  300.9 5.3 %emit_outputs.1 = (f32[384,768]{1,0:T(8,128)}, f32[768,768]{1,0:T(8,128)}, f32[768,768]{1,0:T(8,128)}, f32[24,3072]{1,0:T(8,128)}, f32[48,768]{1,0:T(8,128)}, /*...) custom-call(f32[384,768]{1,0:T(8,128)} %get-tuple-element.152.gi_fro, ...), custom_call_target="tpu_custom_call" | custom-call | tf_op jit(solution)/shard_map/emit_outputs/pallas_call | solution.py:1538
